TPU v7x, 512 devices: a whole 4x4x16 slice. The times are simulated.
512 devices in a mesh: seg: 128 (over x, z, core), lag: 4 (over y).
Axes of the slice: x: 4, y: 4, z: 16, core: 2. Of those that a mesh axis runs over, the one named last changes fastest.
Arguments:
- actuator_input: bfloat16 [393216, 256], P('seg'), may hold values from -24 to 24
- sensor_output: bfloat16 [393216, 2048], P('seg', 'lag'), may hold values from -6 to 6
- run_lengths: int32 [64], replicated, may hold values from 1 to 12288, 393216 in all
- lag_offsets: int32 [2], replicated, may hold values from 0 to 1022, as said below
Outputs:
- markov: float32 [256, 4, 2048], P('seg', 'lag')
Inputs may be any that keep to these rules, and one draw needn't show every extreme that they name: `run_lengths`: the 64 lengths add up to 393216; at least one equals 12288. `lag_offsets`: at least one block starts at 1022.
All inputs are finite; a program needn't handle non-finite values.
Results may differ from a plain program's by a relative error of at most 0.0003.
Values may be sent and summed in bfloat16 or wider, within the bound.
A program may use at most 64 MiB of HBM per device.

v0:
```python
import math

import jax
import jax.numpy as jnp
from jax import lax
from jax.sharding import PartitionSpec as P

LMAX = 1024
LBW = 2
NBLK = 2


def shifted_2(value, axis, steps):
    count = lax.axis_size(axis)
    initial, last = (max(0, -steps), min(count, count - steps))
    return lax.ppermute(value, axis, [(source, source + steps) for source in range(initial, last)])


def segment_ids(run_lengths, start_row, row_count):
    run_ends = jnp.cumsum(run_lengths)
    places = start_row + jnp.arange(row_count, dtype=jnp.int32)
    return jnp.sum((run_ends[None, :] <= places[:, None]).astype(jnp.int32), axis=1)


def product_over_time(masked, shifted):
    return lax.dot_general(
        masked, shifted, (((0,), (0,)), ((), ())), preferred_element_type=jnp.float32
    )


def per_device(actuator_input, sensor_output, run_lengths, lag_offsets):
    samples = actuator_input.shape[0]
    devices_seg = lax.axis_size("seg")
    scaling = 1.0 / math.sqrt(samples * devices_seg)
    start_row = lax.axis_index("seg") * samples
    halo_rows = shifted_2(sensor_output[:LMAX], "seg", -1)
    idents = segment_ids(run_lengths, start_row, samples + LMAX)
    own_ids = idents[:samples]
    shifts = [lag_offsets[blk_num] + lag_step for blk_num in range(NBLK) for lag_step in range(LBW)]
    joined = jnp.concatenate([sensor_output, halo_rows], axis=0)

    def lag_term(columns, lag_value):
        shifted = lax.dynamic_slice_in_dim(joined, lag_value, samples, 0)
        shifted_ids = lax.dynamic_slice_in_dim(idents, lag_value, samples, 0)
        masked = jnp.where((own_ids == shifted_ids)[:, None], columns, jnp.zeros_like(columns))
        return product_over_time(masked, shifted)

    columns = actuator_input
    whole_terms = jnp.stack([lag_term(columns, lag_value) for lag_value in shifts], axis=1)
    owned_terms = lax.all_to_all(whole_terms, "lag", split_axis=1, concat_axis=2, tiled=True)
    result_rows = lax.psum_scatter(owned_terms, "seg", scatter_dimension=0, tiled=True)
    return result_rows * scaling


def solution(mesh):
    return jax.shard_map(
        per_device,
        mesh=mesh,
        in_specs=(P("seg", None), P("seg", "lag"), P(), P()),
        out_specs=P("seg", "lag", None),
        check_vma=False,
    )
```

profile of v0, /device:TPU:1, one launch (start us, length us, event | category | flops | bytes accessed | tf_op | source)
XLA Modules:
  0.0 428.9 jit_solution(18013648685740302071)
XLA Ops:
  6.5 0.0 copy-start
  6.5 0.0 copy-start.1
  6.5 0.0 all-reduce.3.cloned.1.call-start
  6.5 1.3 slice.16
  7.9 8.8 %collective-permute-start = (bf16[1024,512]{1,0:T(8,128)(2,1)S(1)}, bf16[1024,512]{1,0:T(8,128)(2,1)S(1)}, u32[]{:S(2)}, u32[]{:S(2)}) collective-permute-start(bf16[1024,512]{1,0:T(8,128)(2,1)S(1)} %slice.16), channel_id=1, source_target_pairs={{4,0},{8,4},{12,8},{16,12},{20,16},{24,20},{28,24},{32,28},{36,32}... | collective-permute-start | bytes 3145736 | tf_op jit(solution)/shard_map/ppermute | solution.py:16
  16.7 0.0 copy-done
  16.7 0.7 fusion.48
  22.7 0.0 copy-done.1
  22.7 0.1 copy.12
  22.8 0.1 reduce-window.8
  22.9 0.1 reduce
  24.4 0.2 convert_reduce_fusion
  24.6 0.1 dynamic-slice_compare_fusion.3
  24.7 2.1 constant_dynamic-update-slice_fusion.1
  26.8 0.0 copy-start.2
  26.8 0.0 collective-permute-done
  26.8 0.1 constant_dynamic-update-slice_fusion
  26.9 1.3 copy-done.2
  28.2 2.0 fusion.31
  30.2 2.0 fusion.26
  32.2 2.0 fusion.21
  34.1 2.0 fusion.16
  36.1 0.2 pad_maximum_fusion
  36.3 29.1 %all_to_all.12 = f32[256,4,512]{2,0,1:T(8,128)S(1)} all-to-all(f32[256,4,512]{2,0,1:T(8,128)S(1)} %pad_maximum_fusion), channel_id=1, replica_groups=mesh['seg'=128,'lag'=4] {'lag'}, dimensions={1} | all-to-all | bytes 4194304 | tf_op jit(solution)/shard_map/all_to_all | solution.py:50
  65.4 1.8 copy.13
  67.2 6.1 %copy.14 = f32[256,1,2048]{2,1,0:T(1,128)} copy(f32[256,1,2048]{0,2,1:T(8,128)} %bitcast.13) | data formatting | bytes 4194304 | tf_op jit(solution)/shard_map/all_to_all | solution.py:50
  73.3 0.0 all-reduce.3.cloned.1.call-update
  73.3 1.3 dynamic-slice
  75.3 345.5 %all-reduce.3.cloned.1.call-done = f32[256,1,2048]{2,1,0:T(1,128)} async-done(((f32[256,1,2048]{2,1,0:T(1,128)}), f32[256,1,2048]{2,1,0:T(1,128)}) %all-reduce.3.cloned.1.call-update) | async-done | bytes 2097168
  420.8 1.3 dynamic-slice_multiply_fusion
  (1 shorter events, 0.0 us)
Async XLA Ops:
  6.5 10.1 %copy-start = (s32[2]{0:T(128)S(1)}, s32[2]{0:T(128)}, u32[]{:S(2)}) copy-start(s32[2]{0:T(128)} %param.7) | copy-start | bytes 28
  6.5 16.2 %copy-start.1 = (s32[64]{0:T(128)S(1)}, s32[64]{0:T(128)}, u32[]{:S(2)}) copy-start(s32[64]{0:T(128)} %param.6) | copy-start | bytes 772
  6.5 414.2 %all-reduce.3.cloned.1.call-start = ((), (), s32[]{:S(2)}) async-start(), calls=%async_computation.1 | async-start | bytes 4194304
  7.9 18.9 %collective-permute-start = (bf16[1024,512]{1,0:T(8,128)(2,1)S(1)}, bf16[1024,512]{1,0:T(8,128)(2,1)S(1)}, u32[]{:S(2)}, u32[]{:S(2)}) collective-permute-start(bf16[1024,512]{1,0:T(8,128)(2,1)S(1)} %slice.16), channel_id=1, source_target_pairs={{4,0},{8,4},{12,8},{16,12},{20,16},{24,20},{28,24},{32,28},{36,32}... | collective-permute-start | bytes 3145736 | tf_op jit(solution)/shard_map/ppermute | solution.py:16
  26.8 1.4 copy-start.2
Sparse Core Ops, SparseCore 0:
  73.5 347.2 all-reduce.2
where the time goes:
time: 430 us; the launch traced here: 429 us
  waiting for transfers between devices  346 us (80%)
  blocking collectives  29.1 us (7%)
  between operations  20.9 us (5%)
  local copies, waits for them, and re-layouts  14.8 us (3%)
  starting transfers between devices  8.79 us (2%)
  matrix products  7.88 us (2%)
    unnamed x2, waiting for transfers between devices  346 us
    all_to_all x1, blocking collectives, per_device(): lax.all_to_all(whole_terms, 'lag', split_axis=1, concat_axis=2, tiled=True)  29.1 us
    ppermute x1, starting transfers between devices, shifted_2(): lax.ppermute(value, axis, [(source, source + steps) for source in range(i...  8.79 us
  transfers between devices with their start and end apart: 2, of which 1 were waited for; matrix products, arithmetic and copies ran while one was open for 1% of the time, Pallas kernels for 0%

commit v1 on v0

v1 whole, which is shorter than its diff:
```python
import math

import jax
import jax.numpy as jnp
import numpy as np
from jax import lax
from jax.experimental import pallas as pl
from jax.experimental.pallas import tpu as pltpu
from jax.sharding import PartitionSpec as P

LMAX = 1024
LBW = 2
NBLK = 2
NX, NZ, NY, NC = 4, 16, 4, 2
ZL, ZH = 4, 4
F32 = jnp.float32


def device_at(x, z, c, y):
    return (lax.rem(x, NX) * (NZ * NC) + lax.rem(z, NZ) * NC + c, y)


def sums_kernel(part, out, acc, pair, a1, b1, b1h, sa, sb, a2, a2h, b2, stage, fin,
                pair_s, pair_r, a1_s, a1_r, b1_s, b1_r, a2_s, a2_r, b2_s, b2_r, fin_s, fin_r):
    seg, y = lax.axis_index("seg"), lax.axis_index("lag")
    x, z, c = seg // (NZ * NC), lax.rem(seg // NC, NZ), lax.rem(seg, NC)
    zl, zh = lax.rem(z, ZL), z // ZL
    near = [(-1, 0), (1, 1), (2, 2), (-2, 3)]

    def remote(src, dst, send, recv, device):
        return pltpu.make_async_remote_copy(
            src_ref=src, dst_ref=dst, send_sem=send, recv_sem=recv,
            device_id=device, device_id_type=pl.DeviceIdType.MESH)

    barrier = pltpu.get_barrier_semaphore()

    def greet(device):
        pl.semaphore_signal(barrier, inc=1, device_id=device, device_id_type=pl.DeviceIdType.MESH)

    at_home = c == y // 2
    with jax.named_scope("greeting"):
        greet(device_at(x, z, 1 - c, y))
        for dx in range(1, NX):
            greet(device_at(x + dx, z, c, y))
        for step, _ in near:
            greet(device_at(x, z + step + NZ, c, y))
        for q in range(ZH):
            for yy in range(NY):
                source = device_at(x, z + ZL * q, y // 2, lax.rem(y + yy, NY))
                if q == 0 and yy == 0:
                    @pl.when(jnp.logical_not(at_home))
                    def _():
                        greet(source)
                else:
                    greet(source)
        pl.semaphore_wait(barrier, 24 - at_home.astype(jnp.int32))

    waits = []
    with jax.named_scope("pair"):
        pairs = []
        for lag in range(2):
            copy = remote(part.at[2 * (1 - c) + lag], pair.at[lag], pair_s.at[lag], pair_r.at[lag],
                          device_at(x, z, 1 - c, y))
            copy.start()
            pairs.append(copy)
        waits += pairs

    def add_pair(lag):
        @pl.loop(0, NX * ZL)
        def _(i):
            xx, zz = i // ZL, lax.rem(i, ZL)
            acc[lag, xx, zz] = part[2 * c + lag, xx, zz] + pair[lag, xx, zz]

    with jax.named_scope("first"):
        pairs[0].wait_recv()
        add_pair(0)
        x_copies = []
        for dx in (2, 1, 3):
            copy = remote(acc.at[0, lax.rem(x + dx, NX)], a1.at[dx - 1], a1_s.at[dx - 1], a1_r.at[dx - 1],
                          device_at(x + dx, z, c, y))
            copy.start()
            x_copies.append(copy)
        pairs[1].wait_recv()
        add_pair(1)
        z_copies = []
        for step, slot in reversed(near):
            kind = lax.rem(z + step + NZ, ZL)
            if slot < 2:
                src, dst = acc.at[1, :, kind], b1.at[slot]
            else:
                src, dst = acc.at[1, 2 * (slot - 2):2 * (slot - 1), kind], b1h.at[slot - 2]
            copy = remote(src, dst, b1_s.at[slot], b1_r.at[slot], device_at(x, z + step + NZ, c, y))
            copy.start()
            z_copies.append(copy)
        waits += x_copies + z_copies

    with jax.named_scope("second"):
        for copy in x_copies:
            copy.wait_recv()
        for zz in range(ZL):
            sa[zz] = (acc[0, x, zz] + a1[0, zz]) + (a1[1, zz] + a1[2, zz])
        copies_a = []
        for step, slot in reversed(near):
            kind = lax.rem(z + step + NZ, ZL)
            if slot < 2:
                src, dst = sa.at[kind], a2.at[slot]
            else:
                src, dst = sa.at[kind, 8 * (slot - 2):8 * (slot - 1)], a2h.at[slot - 2]
            copy = remote(src, dst, a2_s.at[slot], a2_r.at[slot], device_at(x, z + step + NZ, c, y))
            copy.start()
            copies_a.append(copy)
        for copy in z_copies:
            copy.wait_recv()
        for xx in range(NX):
            sb[xx] = (acc[1, xx, zl] + b1[0, xx]) + (b1[1, xx] + b1h[xx // 2, xx % 2])
        copies_b = []
        for dx in (2, 1, 3):
            copy = remote(sb.at[lax.rem(x + dx, NX)], b2.at[dx - 1], b2_s.at[dx - 1], b2_r.at[dx - 1],
                          device_at(x + dx, z, c, y))
            copy.start()
            copies_b.append(copy)
        waits += copies_a + copies_b

    def send_last(lag):
        for q in (2, 1, 3, 0):
            to_zh = lax.rem(zh + q, ZH)
            for cc in range(NC):
                n = (lag * ZH + q) * NC + cc
                src, dst = stage.at[lag, to_zh, cc], fin.at[zh, y]
                to = device_at(x, z + ZL * q, cc, 2 * c + lag)
                copy = remote(src, dst, fin_s.at[n], fin_r, to)
                if q == 0:
                    mine = (cc == c) & (y == 2 * c + lag)

                    @pl.when(mine)
                    def _():
                        pltpu.make_async_copy(src, dst, fin_r).start()

                    @pl.when(jnp.logical_not(mine))
                    def _():
                        copy.start()
                    last.append((copy, mine))
                else:
                    copy.start()
                    last.append((copy, None))

    with jax.named_scope("third"):
        last = []
        for copy in copies_a:
            copy.wait_recv()
        for half in range(2):
            rows = slice(8 * half, 8 * half + 8)
            total = (sa[zl, rows] + a2[0, rows]) + (a2[1, rows] + a2h[half])
            for k in range(4):
                stage[0, 2 * half + k // 2, k % 2] = total[2 * k:2 * k + 2]
        send_last(0)
        for copy in copies_b:
            copy.wait_recv()
        for half in range(2):
            rows = slice(8 * half, 8 * half + 8)
            total = (sb[x, rows] + b2[0, rows]) + (b2[1, rows] + b2[2, rows])
            for k in range(4):
                stage[1, 2 * half + k // 2, k % 2] = total[2 * k:2 * k + 2]
        send_last(1)

    with jax.named_scope("result"):
        pltpu.make_async_copy(fin, fin, fin_r).wait()
        for yy in range(NY):
            total = (fin[0, yy] + fin[1, yy]) + (fin[2, yy] + fin[3, yy])
            for j in range(2):
                out[j, :, 512 * yy:512 * (yy + 1)] = total[j:j + 1]
        for copy in waits:
            copy.wait_send()
        for copy, mine in last:
            if mine is None:
                copy.wait_send()
            else:
                pl.when(jnp.logical_not(mine))(copy.wait_send)


def summed(part):
    dma = pltpu.SemaphoreType.DMA
    vmem = pltpu.VMEM
    return pl.pallas_call(
        sums_kernel,
        out_shape=jax.ShapeDtypeStruct((2, 1, 2048), F32),
        in_specs=[pl.BlockSpec(memory_space=pltpu.VMEM)],
        out_specs=pl.BlockSpec(memory_space=pltpu.VMEM),
        scratch_shapes=[
            vmem((2, NX, ZL, 16, 512), F32), vmem((2, NX, ZL, 16, 512), F32),
            vmem((3, ZL, 16, 512), F32), vmem((2, NX, 16, 512), F32), vmem((2, 2, 16, 512), F32),
            vmem((ZL, 16, 512), F32), vmem((NX, 16, 512), F32),
            vmem((2, 16, 512), F32), vmem((2, 8, 512), F32), vmem((3, 16, 512), F32),
            vmem((2, ZH, NC, 2, 512), F32), vmem((ZH, NY, 2, 512), F32),
            dma((2,)), dma((2,)), dma((3,)), dma((3,)), dma((4,)), dma((4,)), dma((4,)), dma((4,)),
            dma((3,)), dma((3,)), dma((16,)), dma,
        ],
        compiler_params=pltpu.CompilerParams(collective_id=0, has_side_effects=True,
                                             vmem_limit_bytes=24 << 20),
        name="sums",
    )(part)


def order_of_actuators():
    m = np.arange(256).reshape(NX, ZH, ZL, NC * 2)
    return m.transpose(0, 2, 1, 3).reshape(-1)


def per_device(actuator_input, sensor_output, run_lengths, lag_offsets):
    samples, actuators = actuator_input.shape
    devices_seg = lax.axis_size("seg")
    scaling = 1.0 / math.sqrt(samples * devices_seg)
    start_row = lax.axis_index("seg") * samples
    chosen = jnp.asarray(np.eye(actuators, dtype=np.float32)[:, order_of_actuators()], jnp.bfloat16)
    ordered = jnp.dot(actuator_input, chosen, preferred_element_type=F32).astype(jnp.bfloat16)
    tail = lax.ppermute(ordered[samples - LMAX:], "seg", [(i, i + 1) for i in range(devices_seg - 1)])
    number = run_lengths.shape[0]
    upto = jnp.arange(number)[None, :] <= jnp.arange(number)[:, None]
    run_ends = jnp.sum(jnp.where(upto, run_lengths[None, :], 0), axis=1)
    places = start_row - LMAX + jnp.arange(samples + LMAX, dtype=jnp.int32)
    idents = jnp.sum((run_ends[None, :] <= places[:, None]).astype(jnp.int32), axis=1)
    joined = jnp.concatenate([tail, ordered], axis=0)

    def lag_term(lag_value):
        begin = LMAX - lag_value
        shifted = lax.dynamic_slice_in_dim(joined, begin, samples, 0, allow_negative_indices=False)
        shifted_ids = lax.dynamic_slice_in_dim(idents, begin, samples, 0, allow_negative_indices=False)
        masked = jnp.where((idents[LMAX:] == shifted_ids)[:, None], shifted, jnp.zeros_like(shifted))
        return lax.dot_general(masked, sensor_output, (((0,), (0,)), ((), ())), preferred_element_type=F32)

    shifts = [lag_offsets[blk] + step for blk in range(NBLK) for step in range(LBW)]
    part = jnp.stack([lag_term(lag_value) for lag_value in shifts])
    return summed(part.reshape(4, NX, ZL, 16, 512)) * scaling


def solution(mesh):
    return jax.shard_map(
        per_device,
        mesh=mesh,
        in_specs=(P("seg", None), P("seg", "lag"), P(), P()),
        out_specs=P("seg", "lag", None),
        check_vma=False,
    )
```

time: 430 us -> 66.3 us (0.15)
  waiting for transfers between devices: 346 us -> 2.6 us
  Pallas kernels: 0 us -> 40.2 us
  blocking collectives: 29.1 us -> 0 us
  between operations: 20.9 us -> 2.82 us
  local copies, waits for them, and re-layouts: 14.8 us -> 2.66 us
    unnamed x2 -> x0, waiting for transfers between devices: 346 us -> none
    pallas_call x0 -> x1, Pallas kernels: none -> 40.2 us  [summed(): pl.pallas_call(sums_kernel, out_shape=jax.ShapeDtypeStruct((2, 1, 2048),...]
    all_to_all x1 -> x0, blocking collectives: 29.1 us -> none  [per_device(): lax.all_to_all(whole_terms, 'lag', split_axis=1, concat_axis=2, tiled=True)]
    all_to_all x2 -> x0, local copies, waits for them, and re-layouts: 7.94 us -> none  [per_device(): lax.all_to_all(whole_terms, 'lag', split_axis=1, concat_axis=2, tiled=True)]
    dot_general x4 -> x5, matrix products: 7.88 us -> 11.5 us  [the longest x4 9.21 us: lag_term(): lax.dot_general(masked, sensor_output, (((0,), (0,)), ((), ())), preferre...]
  transfers between devices with their start and end apart: 2 -> 1, of which waited for: 1 -> 1; matrix products, arithmetic and copies ran while one was open for 1% -> 2% of each run, Pallas kernels for 0% -> 0%
where the time goes in v1:
time: 66.3 us; the launch traced here: 66 us
  Pallas kernels  40.2 us (61%)
  matrix products  11.5 us (17%)
  starting transfers between devices  4.93 us (7%)
  between operations  2.82 us (4%)
  local copies, waits for them, and re-layouts  2.66 us (4%)
  waiting for transfers between devices  2.6 us (4%)
  other arithmetic  1.3 us (2%)
    pallas_call x1, Pallas kernels, summed(): pl.pallas_call(sums_kernel, out_shape=jax.ShapeDtypeStruct((2, 1, 2048),...  40.2 us
    dot_general x4, matrix products, lag_term(): lax.dot_general(masked, sensor_output, (((0,), (0,)), ((), ())), preferre...  9.21 us
    ppermute x1, starting transfers between devices, per_device(): lax.ppermute(ordered[samples - LMAX:], 'seg', [(i, i + 1) for i in range(...  4.93 us
    ppermute x1, waiting for transfers between devices, per_device(): lax.ppermute(ordered[samples - LMAX:], 'seg', [(i, i + 1) for i in range(...  2.6 us
    dot_general x1, matrix products, per_device(): jnp.dot(actuator_input, chosen, preferred_element_type=F32)  2.25 us
  transfers between devices with their start and end apart: 1, of which 1 were waited for; matrix products, arithmetic and copies ran while one was open for 2% of the time, Pallas kernels for 0%

profile of v1, /device:TPU:1, one launch (start us, length us, event | category | flops | bytes accessed | tf_op | source)
XLA Modules:
  0.0 66.0 jit_solution(16113224187472891578)
XLA Ops:
  0.0 0.0 copy-start
  0.0 0.0 copy-start.3
  0.0 0.0 copy-start.4
  0.0 2.2 %fusion = bf16[3072,256]{0,1:T(8,128)(2,1)S(1)} fusion(bf16[256,256]{1,0:T(8,128)(2,1)} %constant.28.clone, bf16[3072,256]{1,0:T(8,128)(2,1)} %param.5), kind=kOutput, calls=%fused_computation.5 | convolution fusion | flops 403439616 | bytes 3276800 | tf_op jit(solution)/shard_map/dot_general | solution.py:215
  2.3 0.0 copy-start.1
  2.3 1.2 %copy-done.1 = bf16[3072,256]{0,1:T(8,128)(2,1)} copy-done((bf16[3072,256]{0,1:T(8,128)(2,1)}, bf16[3072,256]{0,1:T(8,128)(2,1)S(1)}, u32[]{:S(2)}) %copy-start.1) | copy-done | bytes 1572888
  3.4 0.8 %slice.22 = bf16[1024,256]{0,1:T(8,128)(2,1)} slice(bf16[3072,256]{0,1:T(8,128)(2,1)S(1)} %fusion), slice={[2048:3072], [0:256]} | slice | bytes 1048576 | tf_op jit(solution)/shard_map/slice | solution.py:216
  4.3 4.9 %collective-permute-start = (bf16[1024,256]{0,1:T(8,128)(2,1)}, bf16[1024,256]{0,1:T(8,128)(2,1)}, u32[]{:S(2)}, u32[]{:S(2)}) collective-permute-start(bf16[1024,256]{0,1:T(8,128)(2,1)} %slice.22), channel_id=1, source_target_pairs={{0,4},{4,8},{8,12},{12,16},{16,20},{20,24},{24,28},{28,32},{32,36}... | collective-permute-start | bytes 1572872 | tf_op jit(solution)/shard_map/ppermute | solution.py:216
  9.2 0.0 copy-done.3
  9.2 0.7 %fusion.37 = (s32[1]{0:T(128)}, s32[1]{0:T(128)}) fusion(s32[2]{0:T(128)S(1)} %copy-done.3), kind=kLoop, calls=%fused_computation.52 | loop fusion | bytes 16 | tf_op jit(solution)/shard_map/slice | solution.py:231
  12.6 0.0 copy-done.4
  12.6 0.1 select_reduce_fusion
  12.7 0.2 convert_reduce_fusion
  12.9 0.1 dynamic-slice_compare_fusion.3
  13.0 2.6 %collective-permute-done = bf16[1024,256]{0,1:T(8,128)(2,1)} collective-permute-done((bf16[1024,256]{0,1:T(8,128)(2,1)}, bf16[1024,256]{0,1:T(8,128)(2,1)}, u32[]{:S(2)}, u32[]{:S(2)}) %collective-permute-start) | collective-permute-done | bytes 524320 | tf_op jit(solution)/shard_map/ppermute | solution.py:216
  15.6 0.0 copy-done
  15.6 0.0 copy-start.2
  15.6 2.7 %fusion.7 = f32[256,512]{1,0:T(8,128)S(1)} fusion(bf16[3072,512]{1,0:T(8,128)(2,1)S(1)} %copy-done, s32[]{:T(128)} %bitcast, bf16[3072,256]{0,1:T(8,128)(2,1)} %copy-done.1, bf16[1024,256]{0,1:T(8,128)(2,1)} %collective-permute-done, pred[3072]{0:T(1024)(128)(4,1)S(1)} %get-tuple-element.5), kind=kOutput, calls=%fused_computation.16 | convolution fusion | flops 809238528 | bytes 5770244 | tf_op jit(solution)/shard_map/dot_general | solution.py:229
  18.3 0.0 copy-done.2
  18.3 2.0 %fusion.11 = f32[256,512]{1,0:T(8,128)S(1)} fusion(bf16[3072,512]{1,0:T(8,128)(2,1)S(1)} %copy-done, s32[]{:T(128)} %bitcast.3, bf16[3072,256]{0,1:T(8,128)(2,1)S(1)} %copy-done.2, bf16[1024,256]{0,1:T(8,128)(2,1)} %collective-permute-done, pred[3072]{0:T(1024)(128)(4,1)S(1)} %get-tuple-element.7), kind=kOutput, calls=%fused_computation.19 | convolution fusion | flops 809238528 | bytes 5770244 | tf_op jit(solution)/shard_map/dot_general | solution.py:229
  20.4 2.2 %fusion.15 = f32[256,512]{1,0:T(8,128)S(1)} fusion(bf16[3072,512]{1,0:T(8,128)(2,1)S(1)} %copy-done, s32[]{:T(128)} %bitcast.5, bf16[3072,256]{0,1:T(8,128)(2,1)S(1)} %copy-done.2, bf16[1024,256]{0,1:T(8,128)(2,1)} %collective-permute-done, pred[3072]{0:T(1024)(128)(4,1)S(1)} %get-tuple-element.6), kind=kOutput, calls=%fused_computation.22 | convolution fusion | flops 809238528 | bytes 5770244 | tf_op jit(solution)/shard_map/dot_general | solution.py:229
  22.6 2.2 %fusion.3 = f32[256,512]{1,0:T(8,128)S(1)} fusion(bf16[3072,512]{1,0:T(8,128)(2,1)S(1)} %copy-done, s32[]{:T(128)} %bitcast.7, bf16[3072,256]{0,1:T(8,128)(2,1)S(1)} %copy-done.2, bf16[1024,256]{0,1:T(8,128)(2,1)} %collective-permute-done, pred[3072]{0:T(1024)(128)(4,1)S(1)} %get-tuple-element.8), kind=kOutput, calls=%fused_computation.13 | convolution fusion | flops 809238528 | bytes 5770244 | tf_op jit(solution)/shard_map/dot_general | solution.py:229
  24.9 0.3 pad_maximum_fusion.part
  25.1 40.2 %sums.1 = f32[2,1,2048]{2,1,0:T(1,128)S(1)} custom-call(f32[4,4,4,16,512]{4,3,2,1,0:T(8,128)S(1)} %pad_maximum_fusion.part), custom_call_target="tpu_custom_call" | custom-call | tf_op jit(solution)/shard_map/sums/pallas_call | solution.py:184
  65.4 0.6 broadcast_multiply_fusion
  (1 shorter events, 0.0 us)
Async XLA Ops:
  0.0 15.6 %copy-start = (bf16[3072,512]{1,0:T(8,128)(2,1)S(1)}, bf16[3072,512]{1,0:T(8,128)(2,1)}, u32[]{:S(2)}) copy-start(bf16[3072,512]{1,0:T(8,128)(2,1)} %param.6) | copy-start | bytes 9437188
  0.0 9.2 %copy-start.3 = (s32[2]{0:T(128)S(1)}, s32[2]{0:T(128)}, u32[]{:S(2)}) copy-start(s32[2]{0:T(128)} %param.8) | copy-start | bytes 28
  0.0 12.6 %copy-start.4 = (s32[64]{0:T(128)S(1)}, s32[64]{0:T(128)}, u32[]{:S(2)}) copy-start(s32[64]{0:T(128)} %param.7) | copy-start | bytes 772
  2.3 1.2 %copy-start.1 = (bf16[3072,256]{0,1:T(8,128)(2,1)}, bf16[3072,256]{0,1:T(8,128)(2,1)S(1)}, u32[]{:S(2)}) copy-start(bf16[3072,256]{0,1:T(8,128)(2,1)S(1)} %fusion) | copy-start | bytes 4718596
  4.3 11.4 %collective-permute-start = (bf16[1024,256]{0,1:T(8,128)(2,1)}, bf16[1024,256]{0,1:T(8,128)(2,1)}, u32[]{:S(2)}, u32[]{:S(2)}) collective-permute-start(bf16[1024,256]{0,1:T(8,128)(2,1)} %slice.22), channel_id=1, source_target_pairs={{0,4},{4,8},{8,12},{12,16},{16,20},{20,24},{24,28},{28,32},{32,36}... | collective-permute-start | bytes 1572872 | tf_op jit(solution)/shard_map/ppermute | solution.py:216
  15.6 2.7 %copy-start.2 = (bf16[3072,256]{0,1:T(8,128)(2,1)S(1)}, bf16[3072,256]{0,1:T(8,128)(2,1)}, u32[]{:S(2)}) copy-start(bf16[3072,256]{0,1:T(8,128)(2,1)} %copy-done.1) | copy-start | bytes 4718596

commit v2 on v0

v2 whole, which is shorter than its diff:
```python
import math

import jax
import jax.numpy as jnp
from jax import lax
from jax.experimental import pallas as pl
from jax.experimental.pallas import tpu as pltpu
from jax.sharding import PartitionSpec as P

LMAX = 1024
NX, NZ, NY, NC = 4, 16, 4, 2
ZL, ZH = 4, 4
TD, M, W = 3072, 256, 512
LANES = 128
F32, BF16 = jnp.float32, jnp.bfloat16


def device_at(x, z, c, y):
    return (lax.rem(x, NX) * (NZ * NC) + lax.rem(z, NZ) * NC + c, y)


def kernel(actuators, sensors, lengths, lags, out,
           act, sen, turned, halo, mask, shifts, lhs, part,
           pair, acc, a1, b1, b1h, sa, sb, a2, a2h, b2, stage, fin,
           in_sem, halo_s, halo_r, pair_s, pair_r, a1_s, a1_r, b1_s, b1_r,
           a2_s, a2_r, b2_s, b2_r, fin_s, fin_r):
    seg, y = lax.axis_index("seg"), lax.axis_index("lag")
    x, z, c = seg // (NZ * NC), lax.rem(seg // NC, NZ), lax.rem(seg, NC)
    zl, zh = lax.rem(z, ZL), z // ZL
    near = [(-1, 0), (1, 1), (2, 2), (-2, 3)]
    after = (lax.rem(seg + 1, NX * NZ * NC), y)
    before = (lax.rem(seg + NX * NZ * NC - 1, NX * NZ * NC), y)

    def remote(src, dst, send, recv, device):
        return pltpu.make_async_remote_copy(
            src_ref=src, dst_ref=dst, send_sem=send, recv_sem=recv,
            device_id=device, device_id_type=pl.DeviceIdType.MESH)

    barrier = pltpu.get_barrier_semaphore()

    def greet(device):
        pl.semaphore_signal(barrier, inc=1, device_id=device, device_id_type=pl.DeviceIdType.MESH)

    at_home = c == y // 2
    greet(before)
    loads = []
    for n, (src, dst) in enumerate([
            (actuators.at[TD - LMAX:], act.at[TD - LMAX:]), (actuators.at[:TD - LMAX], act.at[:TD - LMAX]),
            (sensors.at[LMAX:], sen.at[LMAX:]), (sensors.at[:LMAX], sen.at[:LMAX])]):
        copy = pltpu.make_async_copy(src, dst, in_sem.at[n])
        copy.start()
        loads.append(copy)
    greet(device_at(x, z, 1 - c, y))
    for dx in range(1, NX):
        greet(device_at(x + dx, z, c, y))
    for step, _ in near:
        greet(device_at(x, z + step + NZ, c, y))
    for q in range(ZH):
        for yy in range(NY):
            source = device_at(x, z + ZL * q, y // 2, lax.rem(y + yy, NY))
            if q == 0 and yy == 0:
                pl.when(jnp.logical_not(at_home))(lambda source=source: greet(source))
            else:
                greet(source)

    row = lax.broadcasted_iota(jnp.int32, (M, M), 0)
    col = lax.broadcasted_iota(jnp.int32, (M, M), 1)
    wanted = ((row >> 5) & 3) * 64 + (row >> 7) * 32 + ((row >> 2) & 1) * 16 + ((row >> 3) & 3) * 4 + (row & 3)
    order = (col == wanted).astype(F32).astype(BF16)

    def turn(rows):
        flat = lax.dot_general(order, act[rows], (((1,), (1,)), ((), ())), preferred_element_type=F32)
        for i in range(4):
            turned[(LMAX + rows.start) // LANES + i] = flat[:, LANES * i:LANES * i + LANES].astype(BF16)

    loads[0].wait()
    for k in range(4, 6):
        turn(slice(512 * k, 512 * k + 512))
    pl.semaphore_wait(barrier, 25 - at_home.astype(jnp.int32))
    halos = []
    for half in range(2):
        copy = remote(turned.at[TD // LANES:, 128 * half:128 * half + 128], halo.at[half], halo_s.at[half],
                      halo_r.at[half], after)
        copy.start()
        halos.append(copy)

    lane = lax.broadcasted_iota(jnp.int32, (8, TD), 1)
    place = seg * TD + lane

    def step_run(b, carry):
        end, begin = carry
        end = end + lengths[b]
        return end, jnp.where(place >= end, end, begin)

    _, begin = lax.fori_loop(0, 64, step_run, (jnp.int32(0), jnp.zeros((8, TD), jnp.int32)), unroll=8)
    since = place - begin
    for k in range(4):
        mask[k] = jnp.where(since >= lags[k // 2] + k % 2, 1.0, 0.0)
    for b in range(2):
        rest = (LMAX - 1 - lags[b]) & (LANES - 1)
        shifts[b] = (row == (col & (LANES - 1)) + rest + jnp.where(col < LANES, 1, 0)).astype(F32).astype(BF16)
    loads[1].wait()
    for k in range(4):
        turn(slice(512 * k, 512 * k + 512))

    def build(half, first, count):
        rows = slice(128 * half, 128 * half + 128)

        @pl.loop(0, 2)
        def _(b):
            tile = (LMAX - 1 - lags[b]) >> 7
            tiles = [turned[tile + first + j, rows] for j in range(count + 1)]
            windows = [jnp.concatenate(tiles[j:j + 2], axis=1) for j in range(count)]
            moved = jnp.dot(jnp.concatenate(windows, axis=0), shifts[b], preferred_element_type=F32)
            for j in range(count):
                cols = slice(LANES * j, LANES * j + LANES)
                for k in range(2):
                    value = moved[128 * j:128 * j + 128, LANES * k:LANES * k + LANES].reshape(16, 8, LANES)
                    keep = mask[2 * b + k, :, LANES * (first + j):LANES * (first + j + 1)]
                    at = pl.ds(pl.multiple_of(b * 256 + 128 * k, 128), 128)
                    lhs[at, cols] = (value * keep[None]).reshape(128, LANES).astype(BF16)

    def own(half):
        build(half, 8, 16)

        @pl.loop(0, 2)
        def _(n):
            cols = pl.ds(pl.multiple_of(n * 256, 256), 256)
            part[half, :, :, :, :, cols] = jnp.dot(
                lhs[...], sen[LMAX:, cols], preferred_element_type=F32).reshape(4, NX, ZL, 8, 256)

    def cross(half):
        halos[half].wait_recv()
        turned[:LMAX // LANES, 128 * half:128 * half + 128] = halo[half]
        build(half, 0, 8)

        @pl.loop(0, 2)
        def _(n):
            cols = pl.ds(pl.multiple_of(n * 256, 256), 256)
            part[half, :, :, :, :, cols] += jnp.dot(
                lhs[:, :LMAX], sen[:LMAX, cols], preferred_element_type=F32).reshape(4, NX, ZL, 8, 256)

    waits = list(halos)
    pairs, x_first, z_first, x_second, z_second = {}, {}, {}, {}, {}

    def send_pair(half):
        pairs[half] = remote(part.at[half, pl.ds(2 * (1 - c), 2)], pair.at[half], pair_s.at[half],
                             pair_r.at[half], device_at(x, z, 1 - c, y))
        pairs[half].start()
        waits.append(pairs[half])

    def send_first(half):
        pairs[half].wait_recv()
        for lag in range(2):
            @pl.loop(0, NX)
            def _(xx):
                acc[half, lag, xx] = part[half, 2 * c + lag, xx] + pair[half, lag, xx]

            copies = []
            if lag == 0:
                for dx in (2, 1, 3):
                    copies.append(remote(acc.at[half, 0, lax.rem(x + dx, NX)], a1.at[half, dx - 1],
                                         a1_s.at[half, dx - 1], a1_r.at[half, dx - 1], device_at(x + dx, z, c, y)))
                x_first[half] = copies
            else:
                for step, slot in reversed(near):
                    kind = lax.rem(z + step + NZ, ZL)
                    if slot < 2:
                        src, dst = acc.at[half, 1, :, kind], b1.at[half, slot]
                    else:
                        src, dst = acc.at[half, 1, 2 * (slot - 2):2 * (slot - 1), kind], b1h.at[half, slot - 2]
                    copies.append(remote(src, dst, b1_s.at[half, slot], b1_r.at[half, slot],
                                         device_at(x, z + step + NZ, c, y)))
                z_first[half] = copies
            for copy in copies:
                copy.start()
            waits.extend(copies)

    def send_second(half):
        for copy in x_first[half]:
            copy.wait_recv()
        for zz in range(ZL):
            sa[half, zz] = (acc[half, 0, x, zz] + a1[half, 0, zz]) + (a1[half, 1, zz] + a1[half, 2, zz])
        copies = []
        for step, slot in reversed(near):
            kind = lax.rem(z + step + NZ, ZL)
            if slot < 2:
                src, dst = sa.at[half, kind], a2.at[half, slot]
            else:
                src, dst = sa.at[half, kind, :, 256 * (slot - 2):256 * (slot - 1)], a2h.at[half, slot - 2]
            copies.append(remote(src, dst, a2_s.at[half, slot], a2_r.at[half, slot],
                                 device_at(x, z + step + NZ, c, y)))
            copies[-1].start()
        z_second[half] = copies
        waits.extend(copies)
        for copy in z_first[half]:
            copy.wait_recv()
        for xx in range(NX):
            sb[half, xx] = ((acc[half, 1, xx, zl] + b1[half, 0, xx])
                            + (b1[half, 1, xx] + b1h[half, xx // 2, xx % 2]))
        copies = []
        for dx in (2, 1, 3):
            copies.append(remote(sb.at[half, lax.rem(x + dx, NX)], b2.at[half, dx - 1], b2_s.at[half, dx - 1],
                                 b2_r.at[half, dx - 1], device_at(x + dx, z, c, y)))
            copies[-1].start()
        x_second[half] = copies
        waits.extend(copies)

    last = []

    def send_third(half):
        for lag in range(2):
            for copy in (z_second, x_second)[lag][half]:
                copy.wait_recv()
            if lag == 0:
                far = jnp.concatenate([a2h[half, 0], a2h[half, 1]], axis=1)
                total = (sa[half, zl] + a2[half, 0]) + (a2[half, 1] + far)
            else:
                total = (sb[half, x] + b2[half, 0]) + (b2[half, 1] + b2[half, 2])
            for k in range(4):
                stage[half, lag, k // 2, k % 2] = total[2 * k:2 * k + 2]
            for zb in range(2):
                for cc in range(NC):
                    n = ((half * 2 + lag) * 2 + zb) * NC + cc
                    to_zh = 2 * half + zb
                    src, dst = stage.at[half, lag, zb, cc], fin.at[zh, y]
                    copy = remote(src, dst, fin_s.at[n], fin_r, device_at(x, ZL * to_zh + zl, cc, 2 * c + lag))
                    mine = (cc == c) & (y == 2 * c + lag) & (zh == to_zh)

                    @pl.when(mine)
                    def _():
                        pltpu.make_async_copy(src, dst, fin_r).start()

                    @pl.when(jnp.logical_not(mine))
                    def _():
                        copy.start()
                    last.append((copy, mine))

    loads[2].wait()
    own(0)
    loads[3].wait()
    cross(0)
    send_pair(0)
    own(1)
    send_first(0)
    cross(1)
    send_pair(1)
    send_first(1)
    send_second(0)
    send_third(0)
    send_second(1)
    send_third(1)
    pltpu.make_async_copy(fin, fin, fin_r).wait()
    for yy in range(NY):
        total = (fin[0, yy] + fin[1, yy]) + (fin[2, yy] + fin[3, yy])
        for j in range(2):
            out[j, :, W * yy:W * (yy + 1)] = total[j:j + 1]
    for copy in waits:
        copy.wait_send()
    for copy, mine in last:
        pl.when(jnp.logical_not(mine))(copy.wait_send)


def per_device(actuator_input, sensor_output, run_lengths, lag_offsets):
    samples = actuator_input.shape[0]
    scaling = 1.0 / math.sqrt(samples * lax.axis_size("seg"))
    dma, vmem = pltpu.SemaphoreType.DMA, pltpu.VMEM
    anywhere, scalars = pl.BlockSpec(memory_space=pl.ANY), pl.BlockSpec(memory_space=pltpu.SMEM)
    sums = pl.pallas_call(
        kernel,
        out_shape=jax.ShapeDtypeStruct((2, 1, NY * W), F32),
        in_specs=[anywhere, anywhere, scalars, scalars],
        out_specs=pl.BlockSpec(memory_space=pltpu.VMEM),
        scratch_shapes=[
            vmem((TD, M), BF16), vmem((TD, W), BF16), vmem(((LMAX + TD) // LANES, M, LANES), BF16),
            vmem((2, LMAX // LANES, 128, LANES), BF16), vmem((4, 8, TD), F32),
            vmem((2, 256, 256), BF16), vmem((512, 2048), BF16),
            vmem((2, 4, NX, ZL, 8, W), F32),
            vmem((2, 2, NX, ZL, 8, W), F32), vmem((2, 2, NX, ZL, 8, W), F32),
            vmem((2, 3, ZL, 8, W), F32), vmem((2, 2, NX, 8, W), F32), vmem((2, 2, 2, 8, W), F32),
            vmem((2, ZL, 8, W), F32), vmem((2, NX, 8, W), F32),
            vmem((2, 2, 8, W), F32), vmem((2, 2, 8, 256), F32), vmem((2, 3, 8, W), F32),
            vmem((2, 2, 2, NC, 2, W), F32), vmem((ZH, NY, 2, W), F32),
            dma((4,)), dma((2,)), dma((2,)), dma((2,)), dma((2,)), dma((2, 3)), dma((2, 3)),
            dma((2, 4)), dma((2, 4)), dma((2, 4)), dma((2, 4)), dma((2, 3)), dma((2, 3)), dma((16,)), dma,
        ],
        compiler_params=pltpu.CompilerParams(collective_id=0, has_side_effects=True,
                                             vmem_limit_bytes=40 << 20),
        name="correlate",
    )(actuator_input, sensor_output, run_lengths, lag_offsets)
    return sums * scaling


def solution(mesh):
    return jax.shard_map(
        per_device,
        mesh=mesh,
        in_specs=(P("seg", None), P("seg", "lag"), P(), P()),
        out_specs=P("seg", "lag", None),
        check_vma=False,
    )
```

time: 430 us -> 51.2 us (0.12)
  waiting for transfers between devices: 346 us -> 0 us
  Pallas kernels: 0 us -> 45.8 us
  blocking collectives: 29.1 us -> 0 us
  between operations: 20.9 us -> 0.01 us
  local copies, waits for them, and re-layouts: 14.8 us -> 4.61 us
  starting transfers between devices: 8.79 us -> 0 us
  matrix products: 7.88 us -> 0 us
    unnamed x2 -> x0, waiting for transfers between devices: 346 us -> none
    pallas_call x0 -> x1, Pallas kernels: none -> 45.8 us  [per_device(): pl.pallas_call(kernel, out_shape=jax.ShapeDtypeStruct((2, 1, NY * W), F32...]
    all_to_all x1 -> x0, blocking collectives: 29.1 us -> none  [per_device(): lax.all_to_all(whole_terms, 'lag', split_axis=1, concat_axis=2, tiled=True)]
    ppermute x1 -> x0, starting transfers between devices: 8.79 us -> none  [shifted_2(): lax.ppermute(value, axis, [(source, source + steps) for source in range(i...]
    all_to_all x2 -> x0, local copies, waits for them, and re-layouts: 7.94 us -> none  [per_device(): lax.all_to_all(whole_terms, 'lag', split_axis=1, concat_axis=2, tiled=True)]
    dot_general x4 -> x0, matrix products: 7.88 us -> none  [product_over_time(): lax.dot_general(masked, shifted, (((0,), (0,)), ((), ())), preferred_elem...]
  transfers between devices with their start and end apart: 2 -> 0, of which waited for: 1 -> 0; matrix products, arithmetic and copies ran while one was open for 1% -> 0% of each run, Pallas kernels for 0% -> 0%
where the time goes in v2:
time: 51.2 us; the launch traced here: 51 us
  Pallas kernels  45.8 us (89%)
  local copies, waits for them, and re-layouts  4.61 us (9%)
  other arithmetic  0.62 us (1%)
    pallas_call x1, Pallas kernels, per_device(): pl.pallas_call(kernel, out_shape=jax.ShapeDtypeStruct((2, 1, NY * W), F32...  45.8 us
    unnamed x8, local copies, waits for them, and re-layouts  4.61 us

profile of v2, /device:TPU:1, one launch (start us, length us, event | category | flops | bytes accessed | tf_op | source)
XLA Modules:
  0.0 51.0 jit_solution(11059605976144729529)
XLA Ops:
  0.0 0.0 copy-start
  0.0 1.9 %copy-done = bf16[3072,512]{1,0:T(8,128)(2,1)S(1)} copy-done((bf16[3072,512]{1,0:T(8,128)(2,1)S(1)}, bf16[3072,512]{1,0:T(8,128)(2,1)}, u32[]{:S(2)}) %copy-start) | copy-done | bytes 3145752
  1.9 0.0 copy-start.1
  1.9 1.4 %copy-done.1 = bf16[3072,256]{1,0:T(8,128)(2,1)S(1)} copy-done((bf16[3072,256]{1,0:T(8,128)(2,1)S(1)}, bf16[3072,256]{1,0:T(8,128)(2,1)}, u32[]{:S(2)}) %copy-start.1) | copy-done | bytes 1572888
  3.3 0.0 copy-start.2
  3.3 0.7 %copy-done.2 = s32[64]{0:T(128)S(1)} copy-done((s32[64]{0:T(128)S(1)}, s32[64]{0:T(128)}, u32[]{:S(2)}) %copy-start.2) | copy-done | bytes 280
  4.0 0.0 copy-start.3
  4.0 0.7 %copy-done.3 = s32[2]{0:T(128)S(1)} copy-done((s32[2]{0:T(128)S(1)}, s32[2]{0:T(128)}, u32[]{:S(2)}) %copy-start.3) | copy-done | bytes 32
  4.6 45.8 %correlate.1 = f32[2,1,2048]{2,1,0:T(1,128)S(1)} custom-call(bf16[3072,256]{1,0:T(8,128)(2,1)S(1)} %copy-done.1, bf16[3072,512]{1,0:T(8,128)(2,1)S(1)} %copy-done, s32[64]{0:T(128)S(1)} %copy-done.2, s32[2]{0:T(128)S(1)} %copy-done.3), custom_call_target="tpu_custom_call" | custom-call | tf_op jit(solution)/shard_map/correlate/pallas_call | solution.py:269
  50.4 0.6 %broadcast_multiply_fusion = f32[2,1,2048]{2,1,0:T(1,128)} fusion(f32[2,1,2048]{2,1,0:T(1,128)S(1)} %correlate.1), kind=kLoop, calls=%fused_computation | loop fusion | flops 4096 | bytes 32768 | tf_op jit(solution)/shard_map/mul | solution.py:291
Async XLA Ops:
  0.0 1.9 %copy-start = (bf16[3072,512]{1,0:T(8,128)(2,1)S(1)}, bf16[3072,512]{1,0:T(8,128)(2,1)}, u32[]{:S(2)}) copy-start(bf16[3072,512]{1,0:T(8,128)(2,1)} %sensors.1) | copy-start | bytes 9437188
  1.9 1.4 %copy-start.1 = (bf16[3072,256]{1,0:T(8,128)(2,1)S(1)}, bf16[3072,256]{1,0:T(8,128)(2,1)}, u32[]{:S(2)}) copy-start(bf16[3072,256]{1,0:T(8,128)(2,1)} %actuators.1) | copy-start | bytes 4718596
  3.3 0.7 %copy-start.2 = (s32[64]{0:T(128)S(1)}, s32[64]{0:T(128)}, u32[]{:S(2)}) copy-start(s32[64]{0:T(128)} %lengths.1) | copy-start | bytes 772
  4.0 0.7 %copy-start.3 = (s32[2]{0:T(128)S(1)}, s32[2]{0:T(128)}, u32[]{:S(2)}) copy-start(s32[2]{0:T(128)} %lags.1) | copy-start | bytes 28

commit v3 on v2

--- a/solution.py
+++ b/solution.py
@@ -19,8 +19,8 @@
     return (lax.rem(x, NX) * (NZ * NC) + lax.rem(z, NZ) * NC + c, y)
 
 
-def kernel(actuators, sensors, lengths, lags, out,
-           act, sen, turned, halo, mask, shifts, lhs, part,
+def kernel(actuators, sensors, run_lengths, lag_offsets, out,
+           lengths, lags, act, sen, turned, halo, mask, shifts, lhs, part,
            pair, acc, a1, b1, b1h, sa, sb, a2, a2h, b2, stage, fin,
            in_sem, halo_s, halo_r, pair_s, pair_r, a1_s, a1_r, b1_s, b1_r,
            a2_s, a2_r, b2_s, b2_r, fin_s, fin_r):
@@ -46,7 +46,8 @@
     loads = []
     for n, (src, dst) in enumerate([
             (actuators.at[TD - LMAX:], act.at[TD - LMAX:]), (actuators.at[:TD - LMAX], act.at[:TD - LMAX]),
-            (sensors.at[LMAX:], sen.at[LMAX:]), (sensors.at[:LMAX], sen.at[:LMAX])]):
+            (sensors.at[LMAX:], sen.at[LMAX:]), (sensors.at[:LMAX], sen.at[:LMAX]),
+            (run_lengths, lengths), (lag_offsets, lags)]):
         copy = pltpu.make_async_copy(src, dst, in_sem.at[n])
         copy.start()
         loads.append(copy)
@@ -84,6 +85,8 @@
         copy.start()
         halos.append(copy)
 
+    loads[4].wait()
+    loads[5].wait()
     lane = lax.broadcasted_iota(jnp.int32, (8, TD), 1)
     place = seg * TD + lane
 
@@ -265,13 +268,14 @@
     samples = actuator_input.shape[0]
     scaling = 1.0 / math.sqrt(samples * lax.axis_size("seg"))
     dma, vmem = pltpu.SemaphoreType.DMA, pltpu.VMEM
-    anywhere, scalars = pl.BlockSpec(memory_space=pl.ANY), pl.BlockSpec(memory_space=pltpu.SMEM)
+    in_hbm = pl.BlockSpec(memory_space=pltpu.HBM)
     sums = pl.pallas_call(
         kernel,
         out_shape=jax.ShapeDtypeStruct((2, 1, NY * W), F32),
-        in_specs=[anywhere, anywhere, scalars, scalars],
+        in_specs=[in_hbm] * 4,
         out_specs=pl.BlockSpec(memory_space=pltpu.VMEM),
         scratch_shapes=[
+            pltpu.SMEM((64,), jnp.int32), pltpu.SMEM((2,), jnp.int32),
             vmem((TD, M), BF16), vmem((TD, W), BF16), vmem(((LMAX + TD) // LANES, M, LANES), BF16),
             vmem((2, LMAX // LANES, 128, LANES), BF16), vmem((4, 8, TD), F32),
             vmem((2, 256, 256), BF16), vmem((512, 2048), BF16),
@@ -281,11 +285,11 @@
             vmem((2, ZL, 8, W), F32), vmem((2, NX, 8, W), F32),
             vmem((2, 2, 8, W), F32), vmem((2, 2, 8, 256), F32), vmem((2, 3, 8, W), F32),
             vmem((2, 2, 2, NC, 2, W), F32), vmem((ZH, NY, 2, W), F32),
-            dma((4,)), dma((2,)), dma((2,)), dma((2,)), dma((2,)), dma((2, 3)), dma((2, 3)),
+            dma((6,)), dma((2,)), dma((2,)), dma((2,)), dma((2,)), dma((2, 3)), dma((2, 3)),
             dma((2, 4)), dma((2, 4)), dma((2, 4)), dma((2, 4)), dma((2, 3)), dma((2, 3)), dma((16,)), dma,
         ],
         compiler_params=pltpu.CompilerParams(collective_id=0, has_side_effects=True,
-                                             vmem_limit_bytes=40 << 20),
+                                             vmem_limit_bytes=56 << 20),
         name="correlate",
     )(actuator_input, sensor_output, run_lengths, lag_offsets)
     return sums * scaling

time: 51.2 us -> 47.1 us (0.920)
  local copies, waits for them, and re-layouts: 4.61 us -> 0 us
  other arithmetic: 0.62 us -> 1.34 us
    unnamed x8 -> x0, local copies, waits for them, and re-layouts: 4.61 us -> none
    mul x1, other arithmetic: 0.62 us -> 1.34 us  [per_device(): return sums * scaling]
where the time goes in v3:
time: 47.1 us; the launch traced here: 46.9 us
  Pallas kernels  45.6 us (97%)
  other arithmetic  1.34 us (3%)
    pallas_call x1, Pallas kernels, per_device(): pl.pallas_call(kernel, out_shape=jax.ShapeDtypeStruct((2, 1, NY * W), F32...  45.6 us
    mul x1, other arithmetic, per_device(): return sums * scaling  1.34 us

profile of v3, /device:TPU:1, one launch (start us, length us, event | category | flops | bytes accessed | tf_op | source)
XLA Modules:
  0.0 46.9 jit_solution(1315970109922126567)
XLA Ops:
  0.0 45.6 %correlate.1 = f32[2,1,2048]{2,1,0:T(1,128)} custom-call(bf16[3072,256]{1,0:T(8,128)(2,1)} %actuators.1, bf16[3072,512]{1,0:T(8,128)(2,1)} %sensors.1, s32[64]{0:T(128)} %run_lengths.1, s32[2]{0:T(128)} %lag_offsets.1), custom_call_target="tpu_custom_call" | custom-call | tf_op jit(solution)/shard_map/correlate/pallas_call | solution.py:272
  45.6 1.3 %broadcast_multiply_fusion = f32[2,1,2048]{2,1,0:T(1,128)} fusion(f32[2,1,2048]{2,1,0:T(1,128)} %correlate.1), kind=kLoop, calls=%fused_computation | loop fusion | flops 4096 | bytes 32768 | tf_op jit(solution)/shard_map/mul | solution.py:295

commit v4 on v3

--- a/solution.py
+++ b/solution.py
@@ -23,7 +23,7 @@
            lengths, lags, act, sen, turned, halo, mask, shifts, lhs, part,
            pair, acc, a1, b1, b1h, sa, sb, a2, a2h, b2, stage, fin,
            in_sem, halo_s, halo_r, pair_s, pair_r, a1_s, a1_r, b1_s, b1_r,
-           a2_s, a2_r, b2_s, b2_r, fin_s, fin_r):
+           a2_s, a2_r, b2_s, b2_r, fin_s, fin_r, told):
     seg, y = lax.axis_index("seg"), lax.axis_index("lag")
     x, z, c = seg // (NZ * NC), lax.rem(seg // NC, NZ), lax.rem(seg, NC)
     zl, zh = lax.rem(z, ZL), z // ZL
@@ -41,7 +41,6 @@
     def greet(device):
         pl.semaphore_signal(barrier, inc=1, device_id=device, device_id_type=pl.DeviceIdType.MESH)
 
-    at_home = c == y // 2
     greet(before)
     loads = []
     for n, (src, dst) in enumerate([
@@ -56,13 +55,22 @@
         greet(device_at(x + dx, z, c, y))
     for step, _ in near:
         greet(device_at(x, z + step + NZ, c, y))
-    for q in range(ZH):
-        for yy in range(NY):
-            source = device_at(x, z + ZL * q, y // 2, lax.rem(y + yy, NY))
-            if q == 0 and yy == 0:
-                pl.when(jnp.logical_not(at_home))(lambda source=source: greet(source))
-            else:
-                greet(source)
+    for yy in range(1, NY):
+        greet(device_at(x, z, c, lax.rem(y + yy, NY)))
+
+    rounds = [
+        [device_at(x, z, 1 - c, y)],
+        [device_at(x, z + 2, c, y), device_at(x, z + NZ - 2, c, y)],
+        [device_at(x, z + 4, c, y), device_at(x, z + NZ - 4, c, y)],
+        [device_at(x, z, c, lax.rem(y + yy, NY)) for yy in range(1, NY)],
+    ]
+
+    def tell(n):
+        for device in rounds[n]:
+            pl.semaphore_signal(told.at[n], inc=1, device_id=device, device_id_type=pl.DeviceIdType.MESH)
+
+    def hear(n):
+        pl.semaphore_wait(told.at[n], len(rounds[n]))
 
     row = lax.broadcasted_iota(jnp.int32, (M, M), 0)
     col = lax.broadcasted_iota(jnp.int32, (M, M), 1)
@@ -77,13 +85,14 @@
     loads[0].wait()
     for k in range(4, 6):
         turn(slice(512 * k, 512 * k + 512))
-    pl.semaphore_wait(barrier, 25 - at_home.astype(jnp.int32))
+    pl.semaphore_wait(barrier, 12)
     halos = []
     for half in range(2):
         copy = remote(turned.at[TD // LANES:, 128 * half:128 * half + 128], halo.at[half], halo_s.at[half],
                       halo_r.at[half], after)
         copy.start()
         halos.append(copy)
+    tell(0)
 
     loads[4].wait()
     loads[5].wait()
@@ -239,17 +248,24 @@
                         copy.start()
                     last.append((copy, mine))
 
+    hear(0)
+    tell(1)
     loads[2].wait()
     own(0)
+    hear(1)
+    tell(2)
     loads[3].wait()
     cross(0)
     send_pair(0)
     own(1)
     send_first(0)
+    hear(2)
+    tell(3)
     cross(1)
     send_pair(1)
     send_first(1)
     send_second(0)
+    hear(3)
     send_third(0)
     send_second(1)
     send_third(1)
@@ -287,6 +303,7 @@
             vmem((2, 2, 2, NC, 2, W), F32), vmem((ZH, NY, 2, W), F32),
             dma((6,)), dma((2,)), dma((2,)), dma((2,)), dma((2,)), dma((2, 3)), dma((2, 3)),
             dma((2, 4)), dma((2, 4)), dma((2, 4)), dma((2, 4)), dma((2, 3)), dma((2, 3)), dma((16,)), dma,
+            pltpu.SemaphoreType.REGULAR((4,)),
         ],
         compiler_params=pltpu.CompilerParams(collective_id=0, has_side_effects=True,
                                              vmem_limit_bytes=56 << 20),

time: 47.1 us -> 42.8 us (0.909)
  Pallas kernels: 45.6 us -> 41.3 us
    pallas_call x1, Pallas kernels: 45.6 us -> 41.3 us  [per_device(): pl.pallas_call(kernel, out_shape=jax.ShapeDtypeStruct((2, 1, NY * W), F32...]
where the time goes in v4:
time: 42.8 us; the launch traced here: 42.7 us
  Pallas kernels  41.3 us (96%)
  other arithmetic  1.34 us (3%)
    pallas_call x1, Pallas kernels, per_device(): pl.pallas_call(kernel, out_shape=jax.ShapeDtypeStruct((2, 1, NY * W), F32...  41.3 us
    mul x1, other arithmetic, per_device(): return sums * scaling  1.34 us

profile of v4, /device:TPU:1, one launch (start us, length us, event | category | flops | bytes accessed | tf_op | source)
XLA Modules:
  0.0 42.7 jit_solution(7931243458109326349)
XLA Ops:
  0.0 41.3 %correlate.1 = f32[2,1,2048]{2,1,0:T(1,128)} custom-call(bf16[3072,256]{1,0:T(8,128)(2,1)} %actuators.1, bf16[3072,512]{1,0:T(8,128)(2,1)} %sensors.1, s32[64]{0:T(128)} %run_lengths.1, s32[2]{0:T(128)} %lag_offsets.1), custom_call_target="tpu_custom_call" | custom-call | tf_op jit(solution)/shard_map/correlate/pallas_call | solution.py:288
  41.3 1.3 %broadcast_multiply_fusion = f32[2,1,2048]{2,1,0:T(1,128)} fusion(f32[2,1,2048]{2,1,0:T(1,128)} %correlate.1), kind=kLoop, calls=%fused_computation | loop fusion | flops 4096 | bytes 32768 | tf_op jit(solution)/shard_map/mul | solution.py:312

commit v5 on v0

v5 whole, which is shorter than its diff:
```python
import math

import jax
import jax.numpy as jnp
from jax import lax
from jax.experimental import pallas as pl
from jax.experimental.pallas import tpu as pltpu
from jax.sharding import PartitionSpec as P

LMAX = 1024
NX, NZ, NY, NC = 4, 16, 4, 2
ZL, ZH = 4, 4
TD, M, W = 3072, 256, 512
LANES = 128
HALO = LMAX // LANES
TILES = TD // LANES
F32, BF16 = jnp.float32, jnp.bfloat16


def device_at(x, z, c, y):
    return (lax.rem(x, NX) * (NZ * NC) + lax.rem(z, NZ) * NC + c, lax.rem(y, NY))


def kernel(actuators, sensors, run_lengths, lag_offsets, out,
           lengths, lags, act, sen, head, turned, far, mask, shifts, lhs, part_out, part, pair, acc,
           a1, b1, b1h, sa, sb, a2, a2h, b2, stage, fin,
           in_sem, halo_s, halo_r, core_s, core_r, a1_s, a1_r, b1_s, b1_r,
           a2_s, a2_r, b2_s, b2_r, fin_s, fin_r, told):
    seg, y = lax.axis_index("seg"), lax.axis_index("lag")
    x, z, c = seg // (NZ * NC), lax.rem(seg // NC, NZ), lax.rem(seg, NC)
    zl, zh = lax.rem(z, ZL), z // ZL
    chips = NX * NZ
    near = [(-1, 0), (1, 1), (2, 2), (-2, 3)]
    sibling = device_at(x, z, 1 - c, y)
    first_core, second_core = c == 0, c == 1

    def remote(src, dst, send, recv, device):
        return pltpu.make_async_remote_copy(
            src_ref=src, dst_ref=dst, send_sem=send, recv_sem=recv,
            device_id=device, device_id_type=pl.DeviceIdType.MESH)

    barrier = pltpu.get_barrier_semaphore()

    def signal(semaphore, device):
        pl.semaphore_signal(semaphore, inc=1, device_id=device, device_id_type=pl.DeviceIdType.MESH)

    signal(barrier, (lax.rem(seg // NC + chips - 1, chips) * NC + 1, y))
    loads = []
    for n, (src, dst) in enumerate([
            (actuators.at[TD - LMAX:], act.at[TD - LMAX:]), (actuators.at[:TD - LMAX], act.at[:TD - LMAX]),
            (run_lengths, lengths), (lag_offsets, lags), (sensors, sen)]):
        copy = pltpu.make_async_copy(src, dst, in_sem.at[n])
        copy.start()
        loads.append(copy)
    one_hop = [device_at(x + 1, z, c, y), device_at(x + NX - 1, z, c, y), device_at(x, z + 1, c, y),
               device_at(x, z + NZ - 1, c, y), device_at(x, z, c, y + 1), device_at(x, z, c, y + NY - 1)]
    for device in [sibling] + one_hop:
        signal(barrier, device)

    rounds = [
        one_hop,
        [sibling],
        [device_at(x, z + 2, c, y), device_at(x, z + NZ - 2, c, y)],
        [device_at(x, z + 4, c, y), device_at(x, z + NZ - 4, c, y)],
        [device_at(x, z, c, y + yy) for yy in range(1, NY)],
    ]

    def tell(n):
        for device in rounds[n]:
            signal(told.at[n], device)

    def hear(n):
        pl.semaphore_wait(told.at[n], len(rounds[n]))

    row = lax.broadcasted_iota(jnp.int32, (M, M), 0)
    col = lax.broadcasted_iota(jnp.int32, (M, M), 1)
    wanted = ((row >> 5) & 3) * 64 + (row >> 7) * 32 + ((row >> 2) & 1) * 16 + ((row >> 3) & 3) * 4 + (row & 3)
    order = (col == wanted).astype(F32).astype(BF16)

    def turn(k):
        flat = lax.dot_general(order, act[512 * k:512 * k + 512], (((1,), (1,)), ((), ())),
                               preferred_element_type=F32)
        for i in range(4):
            for half in range(2):
                turned[HALO + 4 * k + i, half] = (
                    flat[128 * half:128 * half + 128, LANES * i:LANES * i + LANES].astype(BF16))

    loads[0].wait()
    turn(4)
    turn(5)
    pl.semaphore_wait(barrier, 7 + 2 * c)
    to_next = lax.rem(seg // NC + 1, chips) * NC
    halos = [remote(turned.at[TILES:, half], far.at[:HALO], halo_s.at[half], halo_r, (to_next + half, y))
             for half in range(2)]
    to_core = [remote(turned.at[TILES:], turned.at[:HALO], core_s.at[0], core_r.at[0], sibling),
               remote(sensors.at[:LMAX], head, core_s.at[1], core_r.at[1], sibling)]
    own_head = pltpu.make_async_copy(sensors.at[:LMAX], head, in_sem.at[5])

    @pl.when(second_core)
    def _():
        for copy in halos:
            copy.start()

    @pl.when(first_core)
    def _():
        for copy in to_core:
            copy.start()
        own_head.start()

    tell(0)

    lane = lax.broadcasted_iota(jnp.int32, (8, TD + LMAX), 1)
    place = jnp.where(lane < TD, seg * TD + lane, (seg - c) * TD + lane - TD)
    loads[2].wait()
    loads[3].wait()

    def step_run(b, carry):
        end, begin = carry
        end = end + lengths[b]
        return end, jnp.where(place >= end, end, begin)

    _, begin = lax.fori_loop(0, 64, step_run, (jnp.int32(0), jnp.zeros((8, TD + LMAX), jnp.int32)), unroll=8)
    since = place - begin
    for k in range(4):
        mask[k] = jnp.where(since >= lags[k // 2] + k % 2, 1.0, 0.0)
    for b in range(2):
        rest = (LMAX - 1 - lags[b]) & (LANES - 1)
        shifts[b] = (row == (col & (LANES - 1)) + rest + jnp.where(col < LANES, 1, 0)).astype(F32).astype(BF16)
    loads[1].wait()
    for k in range(4):
        turn(k)
    far[HALO:] = jnp.zeros((HALO, 128, LANES), BF16)

    def build(tiles_of, b, mask_at, col_at):
        tile = (LMAX - 1 - lags[b]) >> 7
        tiles = [tiles_of(tile + j) for j in range(HALO + 1)]
        windows = [jnp.concatenate(tiles[j:j + 2], axis=1) for j in range(HALO)]
        moved = jnp.dot(jnp.concatenate(windows, axis=0), shifts[b], preferred_element_type=F32)
        for j in range(HALO):
            for k in range(2):
                value = moved[128 * j:128 * j + 128, LANES * k:LANES * k + LANES].reshape(16, 8, LANES)
                keep = mask[2 * b + k, :, mask_at + LANES * j:mask_at + LANES * (j + 1)]
                lhs[256 * b + 128 * k:256 * b + 128 * (k + 1), col_at + LANES * j:col_at + LANES * (j + 1)] = (
                    (value * keep[None]).reshape(128, LANES).astype(BF16))

    def own(half, into):
        for b in range(2):
            for first in range(0, TILES, HALO):
                build(lambda i, first=first: turned[i + first, half], b, LANES * first, LANES * first)

        @pl.loop(0, 2)
        def _(n):
            cols = pl.ds(pl.multiple_of(n * 256, 256), 256)
            into[:, :, :, :, cols] = jnp.dot(
                lhs[...], sen[:, cols], preferred_element_type=F32).reshape(4, NX, ZL, 8, 256)

    hear(0)
    tell(1)

    @pl.when(first_core)
    def _():
        turned[:HALO] = jnp.zeros((HALO, 2, 128, LANES), BF16)

    @pl.when(second_core)
    def _():
        to_core[0].wait_recv()

    loads[4].wait()
    own(1 - c, part_out)
    pairs = remote(part_out, pair, core_s.at[2], core_r.at[2], sibling)
    pairs.start()
    hear(1)
    tell(2)
    own(c, part)
    hear(2)
    tell(3)
    pairs.wait_recv()

    @pl.loop(0, 4)
    def _(k):
        part[k] = part[k] + pair[k]

    @pl.when(first_core)
    def _():
        own_head.wait()

    @pl.when(second_core)
    def _():
        to_core[1].wait_recv()

    halos[0].wait_recv()

    def cross(b):
        build(lambda i: far[i], b, TD, 0)

        @pl.loop(0, 2)
        def _(n):
            cols = pl.ds(pl.multiple_of(n * 256, 256), 256)
            acc[2 * b:2 * b + 2, :, :, :, cols] = jnp.dot(
                lhs[256 * b:256 * b + 256, :LMAX], head[:, cols],
                preferred_element_type=F32).reshape(2, NX, ZL, 8, 256) + part[2 * b:2 * b + 2, :, :, :, cols]

    cross(0)
    x_first = [remote(acc.at[:2, lax.rem(x + dx, NX)], a1.at[dx - 1], a1_s.at[dx - 1], a1_r.at[dx - 1],
                      device_at(x + dx, z, c, y)) for dx in (2, 1, 3)]
    for copy in x_first:
        copy.start()
    cross(1)
    z_first = []
    for step, slot in reversed(near):
        kind = lax.rem(z + step + NZ, ZL)
        if slot < 2:
            src, dst = acc.at[2:, :, kind], b1.at[slot]
        else:
            src, dst = acc.at[slot, :, kind], b1h.at[slot - 2]
        z_first.append(remote(src, dst, b1_s.at[slot], b1_r.at[slot], device_at(x, z + step + NZ, c, y)))
        z_first[-1].start()
    hear(3)
    tell(4)

    for copy in x_first:
        copy.wait_recv()
    for k in range(2):
        for zz in range(ZL):
            sa[k, zz] = (acc[k, x, zz] + a1[0, k, zz]) + (a1[1, k, zz] + a1[2, k, zz])
    z_second = []
    for step, slot in reversed(near):
        kind = lax.rem(z + step + NZ, ZL)
        if slot < 2:
            src, dst = sa.at[:, kind], a2.at[slot]
        else:
            src, dst = sa.at[slot - 2, kind], a2h.at[slot - 2]
        z_second.append(remote(src, dst, a2_s.at[slot], a2_r.at[slot], device_at(x, z + step + NZ, c, y)))
        z_second[-1].start()
    for copy in z_first:
        copy.wait_recv()
    for k in range(2):
        for xx in range(NX):
            sb[k, xx] = (acc[2 + k, xx, zl] + b1[0, k, xx]) + (b1[1, k, xx] + b1h[k, xx])
    x_second = [remote(sb.at[:, lax.rem(x + dx, NX)], b2.at[dx - 1], b2_s.at[dx - 1], b2_r.at[dx - 1],
                       device_at(x + dx, z, c, y)) for dx in (2, 1, 3)]
    for copy in x_second:
        copy.start()

    last = []

    def send_last(k, zb):
        for cc in range(NC):
            n = (k * 2 + zb) * NC + cc
            src, dst = stage.at[k, zb, cc], fin.at[zh, y]
            copy = remote(src, dst, fin_s.at[n], fin_r, device_at(x, ZL * (2 * c + zb) + zl, cc, k))
            mine = (cc == c) & (y == k) & (zh == 2 * c + zb)

            @pl.when(mine)
            def _():
                pltpu.make_async_copy(src, dst, fin_r).start()

            @pl.when(jnp.logical_not(mine))
            def _():
                copy.start()
            last.append((copy, mine))

    def set_out(k, total):
        for i in range(4):
            stage[k, i // 2, i % 2] = total[2 * i:2 * i + 2]

    hear(4)
    for copy in z_second:
        copy.wait_recv()
    for k in range(2):
        set_out(k, (sa[k, zl] + a2[0, k]) + (a2[1, k] + a2h[k]))
        send_last(k, 0)
    for copy in x_second:
        copy.wait_recv()
    for k in range(2):
        set_out(2 + k, (sb[k, x] + b2[0, k]) + (b2[1, k] + b2[2, k]))
        send_last(2 + k, 0)
    for k in range(4):
        send_last(k, 1)

    pairs.wait_send()
    for copy in x_first + z_first + z_second + x_second:
        copy.wait_send()

    @pl.when(second_core)
    def _():
        for copy in halos:
            copy.wait_send()

    @pl.when(first_core)
    def _():
        for copy in to_core:
            copy.wait_send()

    pltpu.make_async_copy(fin, fin, fin_r).wait()
    for yy in range(NY):
        total = (fin[0, yy] + fin[1, yy]) + (fin[2, yy] + fin[3, yy])
        for j in range(2):
            out[j, :, W * yy:W * (yy + 1)] = total[j:j + 1]
    for copy, mine in last:
        pl.when(jnp.logical_not(mine))(copy.wait_send)


def per_device(actuator_input, sensor_output, run_lengths, lag_offsets):
    samples = actuator_input.shape[0]
    scaling = 1.0 / math.sqrt(samples * lax.axis_size("seg"))
    dma, vmem = pltpu.SemaphoreType.DMA, pltpu.VMEM
    operands = [pltpu.with_memory_space_constraint(operand, pltpu.HBM)
                for operand in (actuator_input, sensor_output, run_lengths, lag_offsets)]
    block = (4, NX, ZL, 8, W)
    sums = pl.pallas_call(
        kernel,
        out_shape=jax.ShapeDtypeStruct((2, 1, NY * W), F32),
        in_specs=[pl.BlockSpec(memory_space=pltpu.HBM)] * 4,
        out_specs=pl.BlockSpec(memory_space=pltpu.VMEM),
        scratch_shapes=[
            pltpu.SMEM((64,), jnp.int32), pltpu.SMEM((2,), jnp.int32),
            vmem((TD, M), BF16), vmem((TD, W), BF16), vmem((LMAX, W), BF16),
            vmem((HALO + TILES, 2, 128, LANES), BF16), vmem((2 * HALO, 128, LANES), BF16),
            vmem((4, 8, TD + LMAX), F32), vmem((2, 256, 256), BF16), vmem((512, TD), BF16),
            vmem(block, F32), vmem(block, F32), vmem(block, F32), vmem(block, F32),
            vmem((3, 2, ZL, 8, W), F32), vmem((2, 2, NX, 8, W), F32), vmem((2, NX, 8, W), F32),
            vmem((2, ZL, 8, W), F32), vmem((2, NX, 8, W), F32),
            vmem((2, 2, 8, W), F32), vmem((2, 8, W), F32), vmem((3, 2, 8, W), F32),
            vmem((4, 2, NC, 2, W), F32), vmem((ZH, NY, 2, W), F32),
            dma((6,)), dma((2,)), dma, dma((3,)), dma((3,)), dma((3,)), dma((3,)), dma((4,)), dma((4,)),
            dma((4,)), dma((4,)), dma((3,)), dma((3,)), dma((16,)), dma,
            pltpu.SemaphoreType.REGULAR((5,)),
        ],
        compiler_params=pltpu.CompilerParams(collective_id=0, has_side_effects=True,
                                             vmem_limit_bytes=40 << 20),
        name="correlate",
    )(*operands)
    return sums * scaling


def solution(mesh):
    return jax.shard_map(
        per_device,
        mesh=mesh,
        in_specs=(P("seg", None), P("seg", "lag"), P(), P()),
        out_specs=P("seg", "lag", None),
        check_vma=False,
    )
```

time: 430 us -> 46 us (0.11)
  waiting for transfers between devices: 346 us -> 0 us
  Pallas kernels: 0 us -> 45.3 us
  blocking collectives: 29.1 us -> 0 us
  between operations: 20.9 us -> 0.01 us
  local copies, waits for them, and re-layouts: 14.8 us -> 0 us
  starting transfers between devices: 8.79 us -> 0 us
  matrix products: 7.88 us -> 0 us
    unnamed x2 -> x0, waiting for transfers between devices: 346 us -> none
    pallas_call x0 -> x1, Pallas kernels: none -> 45.3 us  [per_device(): pl.pallas_call(kernel, out_shape=jax.ShapeDtypeStruct((2, 1, NY * W), F32...]
    all_to_all x1 -> x0, blocking collectives: 29.1 us -> none  [per_device(): lax.all_to_all(whole_terms, 'lag', split_axis=1, concat_axis=2, tiled=True)]
    ppermute x1 -> x0, starting transfers between devices: 8.79 us -> none  [shifted_2(): lax.ppermute(value, axis, [(source, source + steps) for source in range(i...]
    all_to_all x2 -> x0, local copies, waits for them, and re-layouts: 7.94 us -> none  [per_device(): lax.all_to_all(whole_terms, 'lag', split_axis=1, concat_axis=2, tiled=True)]
    dot_general x4 -> x0, matrix products: 7.88 us -> none  [product_over_time(): lax.dot_general(masked, shifted, (((0,), (0,)), ((), ())), preferred_elem...]
    unnamed x8 -> x0, local copies, waits for them, and re-layouts: 4.69 us -> none
  transfers between devices with their start and end apart: 2 -> 0, of which waited for: 1 -> 0; matrix products, arithmetic and copies ran while one was open for 1% -> 0% of each run, Pallas kernels for 0% -> 0%
where the time goes in v5:
time: 46 us; the launch traced here: 45.9 us
  Pallas kernels  45.3 us (98%)
  other arithmetic  0.62 us (1%)
    pallas_call x1, Pallas kernels, per_device(): pl.pallas_call(kernel, out_shape=jax.ShapeDtypeStruct((2, 1, NY * W), F32...  45.3 us

profile of v5, /device:TPU:1, one launch (start us, length us, event | category | flops | bytes accessed | tf_op | source)
XLA Modules:
  0.0 45.9 jit_solution(5805393280030245181)
XLA Ops:
  0.0 45.3 %correlate.1 = f32[2,1,2048]{2,1,0:T(1,128)S(1)} custom-call(bf16[3072,256]{1,0:T(8,128)(2,1)} %actuators.1, bf16[3072,512]{1,0:T(8,128)(2,1)} %sensors.1, s32[64]{0:T(128)} %run_lengths.1, s32[2]{0:T(128)} %lag_offsets.1), custom_call_target="tpu_custom_call" | custom-call | tf_op jit(solution)/shard_map/correlate/pallas_call | solution.py:311
  45.3 0.6 %broadcast_multiply_fusion = f32[2,1,2048]{2,1,0:T(1,128)} fusion(f32[2,1,2048]{2,1,0:T(1,128)S(1)} %correlate.1), kind=kLoop, calls=%fused_computation | loop fusion | flops 4096 | bytes 32768 | tf_op jit(solution)/shard_map/mul | solution.py:334

commit v6 on v0

v6 whole, which is shorter than its diff:
```python
import math

import jax
import jax.numpy as jnp
from jax import lax
from jax.experimental import pallas as pl
from jax.experimental.pallas import tpu as pltpu
from jax.sharding import PartitionSpec as P

LMAX = 1024
NX, NZ, NY, NC = 4, 16, 4, 2
ZL, ZH = 4, 4
TD, M, W = 3072, 256, 512
LANES = 128
HALO = LMAX // LANES
TILES = TD // LANES
ORDER = (0, 1, 3, 2)
F32, BF16 = jnp.float32, jnp.bfloat16


def device_at(x, z, c, y):
    return (lax.rem(x, NX) * (NZ * NC) + lax.rem(z, NZ) * NC + c, lax.rem(y, NY))


def kernel(actuators, sensors, run_lengths, lag_offsets, out,
           lengths, lags, act, sen, turned, halo, mask, shifts, lhs, part, pair, acc,
           a1, b1, b1h, sa, sb, a2, a2h, b2, stage, fin,
           in_sem, halo_s, halo_r, pair_s, pair_r, a1_s, a1_r, b1_s, b1_r,
           a2_s, a2_r, b2_s, b2_r, fin_s, fin_r, told):
    seg, y = lax.axis_index("seg"), lax.axis_index("lag")
    x, z, c = seg // (NZ * NC), lax.rem(seg // NC, NZ), lax.rem(seg, NC)
    zl, zh = lax.rem(z, ZL), z // ZL
    after = (lax.rem(seg + 1, NX * NZ * NC), y)
    before = (lax.rem(seg + NX * NZ * NC - 1, NX * NZ * NC), y)
    near = [(-1, 0), (1, 1), (2, 2), (-2, 3)]
    sibling = device_at(x, z, 1 - c, y)

    def remote(src, dst, send, recv, device):
        return pltpu.make_async_remote_copy(
            src_ref=src, dst_ref=dst, send_sem=send, recv_sem=recv,
            device_id=device, device_id_type=pl.DeviceIdType.MESH)

    barrier = pltpu.get_barrier_semaphore()

    def signal(semaphore, device):
        pl.semaphore_signal(semaphore, inc=1, device_id=device, device_id_type=pl.DeviceIdType.MESH)

    signal(barrier, before)
    loads = []
    for n, (src, dst) in enumerate([
            (actuators.at[TD - LMAX:], act.at[TD - LMAX:]), (actuators.at[:TD - LMAX], act.at[:TD - LMAX]),
            (run_lengths, lengths), (lag_offsets, lags),
            (sensors.at[LMAX:], sen.at[LMAX:]), (sensors.at[:LMAX], sen.at[:LMAX])]):
        copy = pltpu.make_async_copy(src, dst, in_sem.at[n])
        copy.start()
        loads.append(copy)
    one_hop = [device_at(x + 1, z, c, y), device_at(x + NX - 1, z, c, y), device_at(x, z + 1, c, y),
               device_at(x, z + NZ - 1, c, y), device_at(x, z, c, y + 1), device_at(x, z, c, y + NY - 1)]
    for device in [sibling] + one_hop:
        signal(barrier, device)

    rounds = [
        one_hop,
        [sibling],
        [device_at(x, z + 2, c, y), device_at(x, z + NZ - 2, c, y)],
        [device_at(x, z + 4, c, y), device_at(x, z + NZ - 4, c, y)],
        [device_at(x, z, c, y + yy) for yy in range(1, NY)],
    ]

    def tell(n):
        for device in rounds[n]:
            signal(told.at[n], device)

    def hear(n):
        pl.semaphore_wait(told.at[n], len(rounds[n]))

    row = lax.broadcasted_iota(jnp.int32, (M, M), 0)
    col = lax.broadcasted_iota(jnp.int32, (M, M), 1)
    wanted = ((row >> 4) & 3) * 64 + (row >> 6) * 16 + ((row >> 2) & 3) * 4 + (row & 3)
    order = (col == wanted).astype(F32).astype(BF16)

    def turn(k):
        flat = lax.dot_general(order, act[512 * k:512 * k + 512], (((1,), (1,)), ((), ())),
                               preferred_element_type=F32)
        for i in range(4):
            turned[HALO + 4 * k + i] = flat[:, LANES * i:LANES * i + LANES].reshape(ZH, 64, LANES).astype(BF16)

    loads[0].wait()
    turn(4)
    turn(5)
    pl.semaphore_wait(barrier, 8)
    halos = {}
    for q in ORDER:
        halos[q] = remote(turned.at[TILES:, q], halo.at[q], halo_s.at[q], halo_r.at[q], after)
        halos[q].start()
    tell(0)

    lane = lax.broadcasted_iota(jnp.int32, (8, TD), 1)
    lag_of_row = lax.broadcasted_iota(jnp.int32, (8, TD), 0) >> 2
    place = seg * TD + lane
    loads[2].wait()
    loads[3].wait()

    def step_run(b, carry):
        end, begin = carry
        end = end + lengths[b]
        return end, jnp.where(place >= end, end, begin)

    _, begin = lax.fori_loop(0, 64, step_run, (jnp.int32(0), jnp.zeros((8, TD), jnp.int32)), unroll=8)
    since = place - begin
    for b in range(2):
        mask[b] = jnp.where(since >= lags[b] + lag_of_row, 1.0, 0.0)
    for b in range(2):
        rest = (LMAX - 1 - lags[b]) & (LANES - 1)
        shifts[b] = (row == (col & (LANES - 1)) + rest + jnp.where(col < LANES, 1, 0)).astype(F32).astype(BF16)
    loads[1].wait()
    for k in range(4):
        turn(k)
    hear(0)
    tell(1)

    first_rows = lax.broadcasted_iota(jnp.int32, (8, 8, LANES), 1) < 4

    def build(q, first, col_at):
        for b in range(2):
            tile = ((LMAX - 1 - lags[b]) >> 7) + first
            tiles = [turned[tile + j, q] for j in range(HALO + 1)]
            windows = [jnp.concatenate(tiles[j:j + 2], axis=1) for j in range(HALO)]
            moved = jnp.dot(jnp.concatenate(windows, axis=0), shifts[b], preferred_element_type=F32)
            for j in range(HALO):
                keep = mask[b, :, LANES * (first + j):LANES * (first + j + 1)][None]
                one, two = [moved[64 * j:64 * j + 64, LANES * k:LANES * k + LANES].reshape(8, 8, LANES)
                            for k in range(2)]
                even = jnp.where(first_rows, one, pltpu.roll(two, 4, 1)) * keep
                odd = jnp.where(first_rows, pltpu.roll(one, 4, 1), two) * keep
                value = jnp.concatenate([even[:, None], odd[:, None]], axis=1).reshape(128, LANES)
                lhs[128 * b:128 * b + 128, col_at + LANES * j:col_at + LANES * (j + 1)] = value.astype(BF16)

    def own(q):
        for first in (HALO, 2 * HALO):
            build(q, first, LANES * (first - HALO))

        @pl.loop(0, 2)
        def _(n):
            cols = pl.ds(pl.multiple_of(n * 256, 256), 256)
            part[q, :, :, :, :, cols] = jnp.dot(
                lhs[...], sen[LMAX:, cols], preferred_element_type=F32).reshape(2, NX, ZL, 8, 256)

    pairs, x_first, z_first, x_second, z_second, last = {}, {}, {}, {}, {}, []

    def cross(q):
        halos[q].wait_recv()
        turned[:HALO, q] = halo[q]
        build(q, 0, 0)

        @pl.loop(0, 2)
        def _(n):
            cols = pl.ds(pl.multiple_of(n * 256, 256), 256)
            part[q, :, :, :, :, cols] += jnp.dot(
                lhs[:, :LMAX], sen[:LMAX, cols], preferred_element_type=F32).reshape(2, NX, ZL, 8, 256)

        pairs[q] = remote(part.at[q, 1 - c], pair.at[q], pair_s.at[q], pair_r.at[q], sibling)
        pairs[q].start()

    def started(copies):
        for copy in copies:
            copy.start()
        return copies

    def send_first(q):
        pairs[q].wait_recv()
        acc[q, :, :, :, :256] = part[q, c, :, :, :, :256] + pair[q, :, :, :, :256]
        x_first[q] = started([
            remote(acc.at[q, lax.rem(x + dx, NX), :, :, :256], a1.at[q, dx - 1], a1_s.at[q, dx - 1],
                   a1_r.at[q, dx - 1], device_at(x + dx, z, c, y)) for dx in (2, 1, 3)])
        acc[q, :, :, :, 256:] = part[q, c, :, :, :, 256:] + pair[q, :, :, :, 256:]
        copies = []
        for step, slot in reversed(near):
            kind = lax.rem(z + step + NZ, ZL)
            if slot < 2:
                src, dst = acc.at[q, :, kind, :, 256:], b1.at[q, slot]
            else:
                src, dst = acc.at[q, 2 * (slot - 2):2 * (slot - 1), kind, :, 256:], b1h.at[q, slot - 2]
            copies.append(remote(src, dst, b1_s.at[q, slot], b1_r.at[q, slot],
                                 device_at(x, z + step + NZ, c, y)))
        z_first[q] = started(copies)

    def send_second(q):
        for copy in x_first[q]:
            copy.wait_recv()
        for zz in range(ZL):
            sa[q, zz] = (acc[q, x, zz, :, :256] + a1[q, 0, zz]) + (a1[q, 1, zz] + a1[q, 2, zz])
        copies = []
        for step, slot in reversed(near):
            kind = lax.rem(z + step + NZ, ZL)
            if slot < 2:
                src, dst = sa.at[q, kind], a2.at[q, slot]
            else:
                src, dst = sa.at[q, kind, :, 128 * (slot - 2):128 * (slot - 1)], a2h.at[q, slot - 2]
            copies.append(remote(src, dst, a2_s.at[q, slot], a2_r.at[q, slot],
                                 device_at(x, z + step + NZ, c, y)))
        z_second[q] = started(copies)
        for copy in z_first[q]:
            copy.wait_recv()
        for xx in range(NX):
            sb[q, xx] = ((acc[q, xx, zl, :, 256:] + b1[q, 0, xx]) + (b1[q, 1, xx] + b1h[q, xx // 2, xx % 2]))
        x_second[q] = started([
            remote(sb.at[q, lax.rem(x + dx, NX)], b2.at[q, dx - 1], b2_s.at[q, dx - 1], b2_r.at[q, dx - 1],
                   device_at(x + dx, z, c, y)) for dx in (2, 1, 3)])

    def send_third(q):
        for copy in z_second[q]:
            copy.wait_recv()
        left = (sa[q, zl] + a2[q, 0]) + (a2[q, 1] + jnp.concatenate([a2h[q, 0], a2h[q, 1]], axis=1))
        for copy in x_second[q]:
            copy.wait_recv()
        right = (sb[q, x] + b2[q, 0]) + (b2[q, 1] + b2[q, 2])
        total = jnp.concatenate([left, right], axis=1)
        for k in range(2):
            for cc in range(NC):
                stage[q, k, cc] = total[4 * k + 2 * cc:4 * k + 2 * cc + 2]
                src, dst = stage.at[q, k, cc], fin.at[zh, y]
                copy = remote(src, dst, fin_s.at[4 * q + 2 * k + cc], fin_r,
                              device_at(x, ZL * q + zl, cc, 2 * c + k))
                mine = (cc == c) & (y == 2 * c + k) & (zh == q)

                @pl.when(mine)
                def _():
                    pltpu.make_async_copy(src, dst, fin_r).start()

                @pl.when(jnp.logical_not(mine))
                def _():
                    copy.start()
                last.append((copy, mine))

    q0, q1, q2, q3 = ORDER
    loads[4].wait()
    own(q0)
    hear(1)
    tell(2)
    own(q1)
    loads[5].wait()
    cross(q0)
    own(q2)
    send_first(q0)
    cross(q1)
    hear(2)
    tell(3)
    own(q3)
    send_first(q1)
    cross(q2)
    send_first(q2)
    send_second(q0)
    cross(q3)
    send_second(q1)
    hear(3)
    tell(4)
    send_first(q3)
    hear(4)
    send_third(q0)
    send_second(q2)
    send_third(q1)
    send_second(q3)
    send_third(q2)
    send_third(q3)
    for q in ORDER:
        for copy in [halos[q], pairs[q]] + x_first[q] + z_first[q] + x_second[q] + z_second[q]:
            copy.wait_send()
    pltpu.make_async_copy(fin, fin, fin_r).wait()
    for yy in range(NY):
        total = (fin[0, yy] + fin[1, yy]) + (fin[2, yy] + fin[3, yy])
        for j in range(2):
            out[j, :, W * yy:W * (yy + 1)] = total[j:j + 1]
    for copy, mine in last:
        pl.when(jnp.logical_not(mine))(copy.wait_send)


def per_device(actuator_input, sensor_output, run_lengths, lag_offsets):
    samples = actuator_input.shape[0]
    scaling = 1.0 / math.sqrt(samples * lax.axis_size("seg"))
    dma, vmem = pltpu.SemaphoreType.DMA, pltpu.VMEM
    operands = [pltpu.with_memory_space_constraint(operand, pltpu.HBM)
                for operand in (actuator_input, sensor_output, run_lengths, lag_offsets)]
    sums = pl.pallas_call(
        kernel,
        out_shape=jax.ShapeDtypeStruct((2, 1, NY * W), F32),
        in_specs=[pl.BlockSpec(memory_space=pltpu.HBM)] * 4,
        out_specs=pl.BlockSpec(memory_space=pltpu.VMEM),
        scratch_shapes=[
            pltpu.SMEM((64,), jnp.int32), pltpu.SMEM((2,), jnp.int32),
            vmem((TD, M), BF16), vmem((TD, W), BF16), vmem((HALO + TILES, ZH, 64, LANES), BF16),
            vmem((ZH, HALO, 64, LANES), BF16), vmem((2, 8, TD), F32), vmem((2, 256, 256), BF16),
            vmem((256, TD - LMAX), BF16), vmem((ZH, 2, NX, ZL, 8, W), F32),
            vmem((ZH, NX, ZL, 8, W), F32), vmem((ZH, NX, ZL, 8, W), F32),
            vmem((ZH, 3, ZL, 8, 256), F32), vmem((ZH, 2, NX, 8, 256), F32), vmem((ZH, 2, 2, 8, 256), F32),
            vmem((ZH, ZL, 8, 256), F32), vmem((ZH, NX, 8, 256), F32),
            vmem((ZH, 2, 8, 256), F32), vmem((ZH, 2, 8, 128), F32), vmem((ZH, 3, 8, 256), F32),
            vmem((ZH, 2, NC, 2, W), F32), vmem((ZH, NY, 2, W), F32),
            dma((6,)), dma((ZH,)), dma((ZH,)), dma((ZH,)), dma((ZH,)), dma((ZH, 3)), dma((ZH, 3)),
            dma((ZH, 4)), dma((ZH, 4)), dma((ZH, 4)), dma((ZH, 4)), dma((ZH, 3)), dma((ZH, 3)), dma((16,)), dma,
            pltpu.SemaphoreType.REGULAR((5,)),
        ],
        compiler_params=pltpu.CompilerParams(collective_id=0, has_side_effects=True,
                                             vmem_limit_bytes=40 << 20),
        name="correlate",
    )(*operands)
    return sums * scaling


def solution(mesh):
    return jax.shard_map(
        per_device,
        mesh=mesh,
        in_specs=(P("seg", None), P("seg", "lag"), P(), P()),
        out_specs=P("seg", "lag", None),
        check_vma=False,
    )
```

time: 430 us -> 41.2 us (0.10)
  waiting for transfers between devices: 346 us -> 0 us
  Pallas kernels: 0 us -> 40.5 us
  blocking collectives: 29.1 us -> 0 us
  between operations: 20.9 us -> 0.01 us
  local copies, waits for them, and re-layouts: 14.8 us -> 0 us
  starting transfers between devices: 8.79 us -> 0 us
  matrix products: 7.88 us -> 0 us
    unnamed x2 -> x0, waiting for transfers between devices: 346 us -> none
    pallas_call x0 -> x1, Pallas kernels: none -> 40.5 us  [per_device(): pl.pallas_call(kernel, out_shape=jax.ShapeDtypeStruct((2, 1, NY * W), F32...]
    all_to_all x1 -> x0, blocking collectives: 29.1 us -> none  [per_device(): lax.all_to_all(whole_terms, 'lag', split_axis=1, concat_axis=2, tiled=True)]
    ppermute x1 -> x0, starting transfers between devices: 8.79 us -> none  [shifted_2(): lax.ppermute(value, axis, [(source, source + steps) for source in range(i...]
    all_to_all x2 -> x0, local copies, waits for them, and re-layouts: 7.94 us -> none  [per_device(): lax.all_to_all(whole_terms, 'lag', split_axis=1, concat_axis=2, tiled=True)]
    dot_general x4 -> x0, matrix products: 7.88 us -> none  [product_over_time(): lax.dot_general(masked, shifted, (((0,), (0,)), ((), ())), preferred_elem...]
    unnamed x8 -> x0, local copies, waits for them, and re-layouts: 4.69 us -> none
  transfers between devices with their start and end apart: 2 -> 0, of which waited for: 1 -> 0; matrix products, arithmetic and copies ran while one was open for 1% -> 0% of each run, Pallas kernels for 0% -> 0%
where the time goes in v6:
time: 41.2 us; the launch traced here: 41.1 us
  Pallas kernels  40.5 us (98%)
  other arithmetic  0.62 us (2%)
    pallas_call x1, Pallas kernels, per_device(): pl.pallas_call(kernel, out_shape=jax.ShapeDtypeStruct((2, 1, NY * W), F32...  40.5 us

profile of v6, /device:TPU:1, one launch (start us, length us, event | category | flops | bytes accessed | tf_op | source)
XLA Modules:
  0.0 41.1 jit_solution(16093050479277183847)
XLA Ops:
  0.0 40.5 %correlate.1 = f32[2,1,2048]{2,1,0:T(1,128)S(1)} custom-call(bf16[3072,256]{1,0:T(8,128)(2,1)} %actuators.1, bf16[3072,512]{1,0:T(8,128)(2,1)} %sensors.1, s32[64]{0:T(128)} %run_lengths.1, s32[2]{0:T(128)} %lag_offsets.1), custom_call_target="tpu_custom_call" | custom-call | tf_op jit(solution)/shard_map/correlate/pallas_call | solution.py:284
  40.5 0.6 %broadcast_multiply_fusion = f32[2,1,2048]{2,1,0:T(1,128)} fusion(f32[2,1,2048]{2,1,0:T(1,128)S(1)} %correlate.1), kind=kLoop, calls=%fused_computation | loop fusion | flops 4096 | bytes 32768 | tf_op jit(solution)/shard_map/mul | solution.py:307

commit v7 on v6

--- a/solution.py
+++ b/solution.py
@@ -61,10 +61,9 @@
 
     rounds = [
         one_hop,
-        [sibling],
-        [device_at(x, z + 2, c, y), device_at(x, z + NZ - 2, c, y)],
+        [device_at(x, z + 2, c, y), device_at(x, z + NZ - 2, c, y), sibling],
         [device_at(x, z + 4, c, y), device_at(x, z + NZ - 4, c, y)],
-        [device_at(x, z, c, y + yy) for yy in range(1, NY)],
+        [sibling] + [device_at(x, z, cc, y + yy) for yy in range(1, NY) for cc in (c, 1 - c)],
     ]
 
     def tell(n):
@@ -236,32 +235,30 @@
     q0, q1, q2, q3 = ORDER
     loads[4].wait()
     own(q0)
+    loads[5].wait()
+    cross(q0)
     hear(1)
     tell(2)
     own(q1)
-    loads[5].wait()
-    cross(q0)
-    own(q2)
     send_first(q0)
     cross(q1)
+    own(q2)
+    send_first(q1)
+    cross(q2)
     hear(2)
     tell(3)
     own(q3)
-    send_first(q1)
-    cross(q2)
+    send_second(q0)
     send_first(q2)
-    send_second(q0)
+    hear(3)
+    send_third(q0)
     cross(q3)
     send_second(q1)
-    hear(3)
-    tell(4)
     send_first(q3)
-    hear(4)
-    send_third(q0)
+    send_third(q1)
     send_second(q2)
-    send_third(q1)
+    send_third(q2)
     send_second(q3)
-    send_third(q2)
     send_third(q3)
     for q in ORDER:
         for copy in [halos[q], pairs[q]] + x_first[q] + z_first[q] + x_second[q] + z_second[q]:
@@ -298,7 +295,7 @@
             vmem((ZH, 2, NC, 2, W), F32), vmem((ZH, NY, 2, W), F32),
             dma((6,)), dma((ZH,)), dma((ZH,)), dma((ZH,)), dma((ZH,)), dma((ZH, 3)), dma((ZH, 3)),
             dma((ZH, 4)), dma((ZH, 4)), dma((ZH, 4)), dma((ZH, 4)), dma((ZH, 3)), dma((ZH, 3)), dma((16,)), dma,
-            pltpu.SemaphoreType.REGULAR((5,)),
+            pltpu.SemaphoreType.REGULAR((4,)),
         ],
         compiler_params=pltpu.CompilerParams(collective_id=0, has_side_effects=True,
                                              vmem_limit_bytes=40 << 20),

time: 41.2 us -> 42.8 us (1.039)
  the two profiles are of different devices: /device:TPU:1 before, /device:TPU:32 now
where the time goes in v7:
time: 42.8 us; the launch traced here: 42.7 us
  Pallas kernels  42 us (98%)
  other arithmetic  0.62 us (1%)
    pallas_call x1, Pallas kernels, per_device(): pl.pallas_call(kernel, out_shape=jax.ShapeDtypeStruct((2, 1, NY * W), F32...  42 us

profile of v7, /device:TPU:32, one launch (start us, length us, event | category | flops | bytes accessed | tf_op | source)
XLA Modules:
  0.0 42.7 jit_solution(14811518233601666046)
XLA Ops:
  0.0 42.0 %correlate.1 = f32[2,1,2048]{2,1,0:T(1,128)S(1)} custom-call(bf16[3072,256]{1,0:T(8,128)(2,1)} %actuators.1, bf16[3072,512]{1,0:T(8,128)(2,1)} %sensors.1, s32[64]{0:T(128)} %run_lengths.1, s32[2]{0:T(128)} %lag_offsets.1), custom_call_target="tpu_custom_call" | custom-call | tf_op jit(solution)/shard_map/correlate/pallas_call | solution.py:281
  42.0 0.6 %broadcast_multiply_fusion = f32[2,1,2048]{2,1,0:T(1,128)} fusion(f32[2,1,2048]{2,1,0:T(1,128)S(1)} %correlate.1), kind=kLoop, calls=%fused_computation | loop fusion | flops 4096 | bytes 32768 | tf_op jit(solution)/shard_map/mul | solution.py:304

commit v8 on v7

--- a/solution.py
+++ b/solution.py
@@ -115,8 +115,6 @@
     loads[1].wait()
     for k in range(4):
         turn(k)
-    hear(0)
-    tell(1)
 
     first_rows = lax.broadcasted_iota(jnp.int32, (8, 8, LANES), 1) < 4
 
@@ -235,25 +233,27 @@
     q0, q1, q2, q3 = ORDER
     loads[4].wait()
     own(q0)
+    hear(0)
+    tell(1)
     loads[5].wait()
     cross(q0)
+    own(q1)
+    send_first(q0)
     hear(1)
     tell(2)
-    own(q1)
-    send_first(q0)
     cross(q1)
     own(q2)
     send_first(q1)
     cross(q2)
+    send_second(q0)
     hear(2)
     tell(3)
     own(q3)
-    send_second(q0)
     send_first(q2)
     hear(3)
     send_third(q0)
+    send_second(q1)
     cross(q3)
-    send_second(q1)
     send_first(q3)
     send_third(q1)
     send_second(q2)

time: 42.8 us -> 41.3 us (0.965)
  the two profiles are of different devices: /device:TPU:32 before, /device:TPU:1 now
where the time goes in v8:
time: 41.3 us; the launch traced here: 40.6 us
  Pallas kernels  39.9 us (97%)
  other arithmetic  0.62 us (2%)
    pallas_call x1, Pallas kernels, per_device(): pl.pallas_call(kernel, out_shape=jax.ShapeDtypeStruct((2, 1, NY * W), F32...  39.9 us

profile of v8, /device:TPU:1, one launch (start us, length us, event | category | flops | bytes accessed | tf_op | source)
XLA Modules:
  0.0 40.6 jit_solution(2858189424775999362)
XLA Ops:
  0.0 39.9 %correlate.1 = f32[2,1,2048]{2,1,0:T(1,128)S(1)} custom-call(bf16[3072,256]{1,0:T(8,128)(2,1)} %actuators.1, bf16[3072,512]{1,0:T(8,128)(2,1)} %sensors.1, s32[64]{0:T(128)} %run_lengths.1, s32[2]{0:T(128)} %lag_offsets.1), custom_call_target="tpu_custom_call" | custom-call | tf_op jit(solution)/shard_map/correlate/pallas_call | solution.py:281
  39.9 0.6 %broadcast_multiply_fusion = f32[2,1,2048]{2,1,0:T(1,128)} fusion(f32[2,1,2048]{2,1,0:T(1,128)S(1)} %correlate.1), kind=kLoop, calls=%fused_computation | loop fusion | flops 4096 | bytes 32768 | tf_op jit(solution)/shard_map/mul | solution.py:304

commit v9 on v8

--- a/solution.py
+++ b/solution.py
@@ -245,20 +245,20 @@
     own(q2)
     send_first(q1)
     cross(q2)
+    own(q3)
     send_second(q0)
     hear(2)
     tell(3)
-    own(q3)
     send_first(q2)
+    cross(q3)
+    send_second(q1)
+    send_first(q3)
     hear(3)
     send_third(q0)
-    send_second(q1)
-    cross(q3)
-    send_first(q3)
+    send_second(q2)
     send_third(q1)
-    send_second(q2)
+    send_second(q3)
     send_third(q2)
-    send_second(q3)
     send_third(q3)
     for q in ORDER:
         for copy in [halos[q], pairs[q]] + x_first[q] + z_first[q] + x_second[q] + z_second[q]:

time: 41.3 us -> 39.7 us (0.961); the launches traced: 40.6 us -> 39.6 us
  Pallas kernels: 39.9 us -> 38.9 us
    pallas_call x1, Pallas kernels: 39.9 us -> 38.9 us  [per_device(): pl.pallas_call(kernel, out_shape=jax.ShapeDtypeStruct((2, 1, NY * W), F32...]
where the time goes in v9:
time: 39.7 us; the launch traced here: 39.6 us
  Pallas kernels  38.9 us (98%)
  other arithmetic  0.62 us (2%)
    pallas_call x1, Pallas kernels, per_device(): pl.pallas_call(kernel, out_shape=jax.ShapeDtypeStruct((2, 1, NY * W), F32...  38.9 us

profile of v9, /device:TPU:1, one launch (start us, length us, event | category | flops | bytes accessed | tf_op | source)
XLA Modules:
  0.0 39.6 jit_solution(2108248610967643092)
XLA Ops:
  0.0 38.9 %correlate.1 = f32[2,1,2048]{2,1,0:T(1,128)S(1)} custom-call(bf16[3072,256]{1,0:T(8,128)(2,1)} %actuators.1, bf16[3072,512]{1,0:T(8,128)(2,1)} %sensors.1, s32[64]{0:T(128)} %run_lengths.1, s32[2]{0:T(128)} %lag_offsets.1), custom_call_target="tpu_custom_call" | custom-call | tf_op jit(solution)/shard_map/correlate/pallas_call | solution.py:281
  38.9 0.6 %broadcast_multiply_fusion = f32[2,1,2048]{2,1,0:T(1,128)} fusion(f32[2,1,2048]{2,1,0:T(1,128)S(1)} %correlate.1), kind=kLoop, calls=%fused_computation | loop fusion | flops 4096 | bytes 32768 | tf_op jit(solution)/shard_map/mul | solution.py:304

commit v10 on v9

--- a/solution.py
+++ b/solution.py
@@ -87,13 +87,6 @@
     loads[0].wait()
     turn(4)
     turn(5)
-    pl.semaphore_wait(barrier, 8)
-    halos = {}
-    for q in ORDER:
-        halos[q] = remote(turned.at[TILES:, q], halo.at[q], halo_s.at[q], halo_r.at[q], after)
-        halos[q].start()
-    tell(0)
-
     lane = lax.broadcasted_iota(jnp.int32, (8, TD), 1)
     lag_of_row = lax.broadcasted_iota(jnp.int32, (8, TD), 0) >> 2
     place = seg * TD + lane
@@ -112,6 +105,13 @@
     for b in range(2):
         rest = (LMAX - 1 - lags[b]) & (LANES - 1)
         shifts[b] = (row == (col & (LANES - 1)) + rest + jnp.where(col < LANES, 1, 0)).astype(F32).astype(BF16)
+    pl.semaphore_wait(barrier, 8)
+    halos = {}
+    for q in ORDER:
+        halos[q] = remote(turned.at[TILES:, q], halo.at[q], halo_s.at[q], halo_r.at[q], after)
+        halos[q].start()
+    tell(0)
+
     loads[1].wait()
     for k in range(4):
         turn(k)
@@ -233,26 +233,26 @@
     q0, q1, q2, q3 = ORDER
     loads[4].wait()
     own(q0)
+    own(q1)
     hear(0)
     tell(1)
     loads[5].wait()
     cross(q0)
-    own(q1)
+    own(q2)
     send_first(q0)
     hear(1)
     tell(2)
     cross(q1)
-    own(q2)
+    own(q3)
     send_first(q1)
     cross(q2)
-    own(q3)
+    cross(q3)
     send_second(q0)
     hear(2)
     tell(3)
     send_first(q2)
-    cross(q3)
+    send_first(q3)
     send_second(q1)
-    send_first(q3)
     hear(3)
     send_third(q0)
     send_second(q2)

time: 39.7 us -> 39.2 us (0.987)
  Pallas kernels: 38.9 us -> 38.5 us
    pallas_call x1, Pallas kernels: 38.9 us -> 38.5 us  [per_device(): pl.pallas_call(kernel, out_shape=jax.ShapeDtypeStruct((2, 1, NY * W), F32...]
where the time goes in v10:
time: 39.2 us; the launch traced here: 39.1 us
  Pallas kernels  38.5 us (98%)
  other arithmetic  0.62 us (2%)
    pallas_call x1, Pallas kernels, per_device(): pl.pallas_call(kernel, out_shape=jax.ShapeDtypeStruct((2, 1, NY * W), F32...  38.5 us

profile of v10, /device:TPU:1, one launch (start us, length us, event | category | flops | bytes accessed | tf_op | source)
XLA Modules:
  0.0 39.1 jit_solution(9062264672708193877)
XLA Ops:
  0.0 38.5 %correlate.1 = f32[2,1,2048]{2,1,0:T(1,128)S(1)} custom-call(bf16[3072,256]{1,0:T(8,128)(2,1)} %actuators.1, bf16[3072,512]{1,0:T(8,128)(2,1)} %sensors.1, s32[64]{0:T(128)} %run_lengths.1, s32[2]{0:T(128)} %lag_offsets.1), custom_call_target="tpu_custom_call" | custom-call | tf_op jit(solution)/shard_map/correlate/pallas_call | solution.py:281
  38.5 0.6 %broadcast_multiply_fusion = f32[2,1,2048]{2,1,0:T(1,128)} fusion(f32[2,1,2048]{2,1,0:T(1,128)S(1)} %correlate.1), kind=kLoop, calls=%fused_computation | loop fusion | flops 4096 | bytes 32768 | tf_op jit(solution)/shard_map/mul | solution.py:304
